TPU v7x, 32 devices: a whole 2x2x4 slice. The times are simulated.
32 devices in a mesh: dp: 8 (over z, y), fsdp: 4 (over x, core).
Axes of the slice: x: 2, y: 2, z: 4, core: 2. Of those that a mesh axis runs over, the one named last changes fastest.
Arguments:
- inputs: bfloat16 [2, 16384, 768], P(None, ('dp', 'fsdp')), may hold values from -6 to 6
- cotangent: bfloat16 [2, 16384, 768], P(None, ('dp', 'fsdp')), may hold values from -6 to 6
- prefix: int32 [2, 16], P(None, 'dp'), may hold values from 102 to 512, as said below
- w_query: bfloat16 [768, 768], P(('dp', 'fsdp')), may hold values from -0.21875 to 0.21875
- w_key: bfloat16 [768, 768], P(('dp', 'fsdp')), may hold values from -0.21875 to 0.21875
- w_value: bfloat16 [768, 768], P(('dp', 'fsdp')), may hold values from -0.21875 to 0.21875
- w_out: bfloat16 [768, 768], P(('dp', 'fsdp')), may hold values from -0.875 to 0.875
- w_up: bfloat16 [768, 3072], P(('dp', 'fsdp')), may hold values from -0.21875 to 0.21875
- w_down: bfloat16 [3072, 768], P(('dp', 'fsdp')), may hold values from -0.109375 to 0.109375
- b_query: bfloat16 [768], P(('dp', 'fsdp')), may hold values from -1.796875 to 1.796875
- b_value: bfloat16 [768], P(('dp', 'fsdp')), may hold values from -1.796875 to 1.796875
- b_out: bfloat16 [768], P(('dp', 'fsdp')), may hold values from -1.796875 to 1.796875
- b_up: bfloat16 [3072], P(('dp', 'fsdp')), may hold values from -1.796875 to 1.796875
- b_down: bfloat16 [768], P(('dp', 'fsdp')), may hold values from -1.796875 to 1.796875
- gain_attn: bfloat16 [768], P(('dp', 'fsdp')), may hold values from 0.5 to 1.5
- shift_attn: bfloat16 [768], P(('dp', 'fsdp')), may hold values from -1.796875 to 1.796875
- gain_ffn: bfloat16 [768], P(('dp', 'fsdp')), may hold values from 0.5 to 1.5
- shift_ffn: bfloat16 [768], P(('dp', 'fsdp')), may hold values from -1.796875 to 1.796875
Outputs:
- layer_out: bfloat16 [2, 16384, 768], P(None, ('dp', 'fsdp'))
- grad_inputs: float32 [2, 16384, 768], P(None, ('dp', 'fsdp'))
- grad_w_query: float32 [768, 768], P(('dp', 'fsdp'))
- grad_w_key: float32 [768, 768], P(('dp', 'fsdp'))
- grad_w_value: float32 [768, 768], P(('dp', 'fsdp'))
- grad_w_out: float32 [768, 768], P(('dp', 'fsdp'))
- grad_w_up: float32 [768, 3072], P(('dp', 'fsdp'))
- grad_w_down: float32 [3072, 768], P(('dp', 'fsdp'))
- grad_b_query: float32 [768], P(('dp', 'fsdp'))
- grad_b_value: float32 [768], P(('dp', 'fsdp'))
- grad_b_out: float32 [768], P(('dp', 'fsdp'))
- grad_b_up: float32 [3072], P(('dp', 'fsdp'))
- grad_b_down: float32 [768], P(('dp', 'fsdp'))
- grad_gain_attn: float32 [768], P(('dp', 'fsdp'))
- grad_shift_attn: float32 [768], P(('dp', 'fsdp'))
- grad_gain_ffn: float32 [768], P(('dp', 'fsdp'))
- grad_shift_ffn: float32 [768], P(('dp', 'fsdp'))
Inputs may be any that keep to these rules, and one draw needn't show every extreme that they name: The bidirectional prefix of sequence s in micro-batch m; it never passes 1024 // 2, so block 1 of every sequence is causal.
All inputs are finite; a program needn't handle non-finite values.
Results may differ from a plain program's by a relative error of at most 0.015.
Values may be sent and summed in bfloat16 or wider, within the bound.
No kernel may reach another device: no remote copies, remote signals or barrier semaphores. Data moves between devices by JAX's collectives and lax.ppermute only.
A program may use at most 256 MiB of HBM per device.

v0:
```python
import jax
import jax.numpy as jnp
from jax import lax
from jax.sharding import PartitionSpec as P

D = 768
FF = 3072
HEADS = 12
GLOBAL = 128


norm_epsilon = 1e-05
score_scale = 0.125
masked_fill = -1e30


def shifted(value, axis, steps):
    count = lax.axis_size(axis)
    leading, last = (max(0, -steps), min(count, count - steps))
    return lax.ppermute(value, axis, [(source, source + steps) for source in range(leading, last)])


def product(left, right):
    return jnp.dot(left, right, preferred_element_type=jnp.float32)


def normalize(values, gain, shift):
    center = jnp.mean(values, -1, keepdims=True)
    centered = values - center
    spread = jnp.mean(centered * centered, -1, keepdims=True)
    inv_std = lax.rsqrt(spread + norm_epsilon)
    normed = centered * inv_std
    return (normed * gain + shift, normed, inv_std)


def normalize_back(grad_out, normed, inv_std, gain):
    grad_norm = grad_out * gain
    return inv_std * (
        grad_norm
        - jnp.mean(grad_norm, -1, keepdims=True)
        - normed * jnp.mean(grad_norm * normed, -1, keepdims=True)
    )


def split_heads(values, groups):
    return jnp.moveaxis(
        values.reshape(values.shape[0], groups, 2, values.shape[1] // (2 * groups)), 1, 0
    )


def join_heads(values):
    return jnp.moveaxis(values, 0, 1).reshape(values.shape[1], -1)


def scores_of(query_group, key_group, allowed):
    raw_scores = jnp.einsum(
        "qhd,khd->hqk", query_group, key_group, preferred_element_type=jnp.float32
    )
    return jnp.where(allowed[None], raw_scores * score_scale, masked_fill)


def body(
    inputs,
    cotangent,
    prefix,
    w_query,
    w_key,
    w_value,
    w_out,
    w_up,
    w_down,
    b_query,
    b_value,
    b_out,
    b_up,
    b_down,
    gain_attn,
    shift_attn,
    gain_ffn,
    shift_ffn,
):
    fsdp_index = lax.axis_index("fsdp")
    first_block = fsdp_index % 2 == 0
    seq_slot = fsdp_index // 2
    groups = HEADS // 2

    def collect():
        return (
            lax.all_gather(w_query, ("dp", "fsdp"), axis=0, tiled=True),
            lax.all_gather(w_key, ("dp", "fsdp"), axis=0, tiled=True),
            lax.all_gather(w_value, ("dp", "fsdp"), axis=0, tiled=True),
            lax.all_gather(w_out, ("dp", "fsdp"), axis=0, tiled=True),
            lax.all_gather(w_up, ("dp", "fsdp"), axis=0, tiled=True),
            lax.all_gather(w_down, ("dp", "fsdp"), axis=0, tiled=True),
            lax.all_gather(b_query, ("dp", "fsdp"), axis=0, tiled=True),
            lax.all_gather(b_value, ("dp", "fsdp"), axis=0, tiled=True),
            lax.all_gather(b_out, ("dp", "fsdp"), axis=0, tiled=True),
            lax.all_gather(b_up, ("dp", "fsdp"), axis=0, tiled=True),
            lax.all_gather(b_down, ("dp", "fsdp"), axis=0, tiled=True),
            lax.all_gather(gain_attn, ("dp", "fsdp"), axis=0, tiled=True),
            lax.all_gather(shift_attn, ("dp", "fsdp"), axis=0, tiled=True),
            lax.all_gather(gain_ffn, ("dp", "fsdp"), axis=0, tiled=True),
            lax.all_gather(shift_ffn, ("dp", "fsdp"), axis=0, tiled=True),
        )

    def micro_step(grad_sum, item):
        tokens, grad_out, prefix_pair = item
        block_rows = tokens.shape[0]
        key_count = GLOBAL + block_rows
        prefix_len = jnp.sum(
            jnp.where(jnp.arange(prefix_pair.shape[0]) == seq_slot, prefix_pair, 0)
        )
        query_pos = lax.broadcasted_iota(jnp.int32, (block_rows, key_count), 0)
        key_pos = lax.broadcasted_iota(jnp.int32, (block_rows, key_count), 1) - GLOBAL
        allowed = jnp.where(
            key_pos < 0,
            jnp.logical_not(first_block),
            (key_pos <= query_pos) | first_block & (key_pos < prefix_len),
        )
        (
            full_query,
            full_key,
            full_value,
            full_out,
            full_up,
            full_down,
            bias_query,
            bias_value,
            bias_out,
            bias_up,
            bias_down,
            gain_one,
            shift_one,
            gain_two,
            shift_two,
        ) = collect()
        gain_onef = gain_one.astype(jnp.float32)
        gain_twof = gain_two.astype(jnp.float32)
        values = tokens.astype(jnp.float32)
        normed_one, unit_one, inv_one = normalize(values, gain_onef, shift_one.astype(jnp.float32))
        normed_low = normed_one.astype(jnp.bfloat16)
        queries = (product(normed_low, full_query) + bias_query.astype(jnp.float32)).astype(
            jnp.bfloat16
        )
        key_local = product(normed_low, full_key).astype(jnp.bfloat16)
        value_local = (product(normed_low, full_value) + bias_value.astype(jnp.float32)).astype(
            jnp.bfloat16
        )
        leading = shifted(jnp.stack([key_local[:GLOBAL], value_local[:GLOBAL]]), "fsdp", 1)
        key_rows = jnp.concatenate([leading[0], key_local], 0)
        value_rows = jnp.concatenate([leading[1], value_local], 0)

        def group_forward(group_items):
            query_group, key_group, value_group = group_items
            scores = scores_of(query_group, key_group, allowed)
            row_top = jnp.max(scores, -1, keepdims=True)
            expon = jnp.exp(scores - row_top)
            row_total = jnp.sum(expon, -1, keepdims=True)
            prob_low = (expon / row_total).astype(jnp.bfloat16)
            attended = jnp.einsum(
                "hqk,khd->qhd", prob_low, value_group, preferred_element_type=jnp.float32
            )
            return (attended, (row_top + jnp.log(row_total))[..., 0])

        query_heads = split_heads(queries, groups)
        key_heads = split_heads(key_rows, groups)
        value_heads = split_heads(value_rows, groups)
        attended, log_total = lax.map(group_forward, (query_heads, key_heads, value_heads))
        attn_low = join_heads(attended).astype(jnp.bfloat16)
        middle = values + product(attn_low, full_out) + bias_out.astype(jnp.float32)
        normed_two, unit_two, inv_two = normalize(middle, gain_twof, shift_two.astype(jnp.float32))
        normed_two_low = normed_two.astype(jnp.bfloat16)
        hidden = product(normed_two_low, full_up) + bias_up.astype(jnp.float32)
        activated, gelu_back = jax.vjp(jax.nn.gelu, hidden)
        act_low = activated.astype(jnp.bfloat16)
        layer_out = (middle + product(act_low, full_down) + bias_down.astype(jnp.float32)).astype(
            jnp.bfloat16
        )
        (
            full_query,
            full_key,
            full_value,
            full_out,
            full_up,
            full_down,
            bias_query,
            bias_value,
            bias_out,
            bias_up,
            bias_down,
            gain_one,
            shift_one,
            gain_two,
            shift_two,
        ) = collect()
        grad_outf = grad_out.astype(jnp.float32)
        grad_b_down = jnp.sum(grad_outf, 0)
        grad_w_down = jnp.einsum("tf,td->fd", act_low, grad_out, preferred_element_type=jnp.float32)
        d_act = jnp.einsum("td,fd->tf", grad_out, full_down, preferred_element_type=jnp.float32)
        d_hidden = gelu_back(d_act)[0].astype(jnp.bfloat16)
        grad_b_up = jnp.sum(d_hidden, 0, dtype=jnp.float32)
        grad_w_up = jnp.einsum(
            "td,tf->df", normed_two_low, d_hidden, preferred_element_type=jnp.float32
        )
        d_normed_two = jnp.einsum(
            "tf,df->td", d_hidden, full_up, preferred_element_type=jnp.float32
        )
        grad_gain_two = jnp.sum(d_normed_two * unit_two, 0)
        grad_shift_two = jnp.sum(d_normed_two, 0)
        d_middle = grad_outf + normalize_back(d_normed_two, unit_two, inv_two, gain_twof)
        d_branch = d_middle.astype(jnp.bfloat16)
        grad_b_out = jnp.sum(d_branch, 0, dtype=jnp.float32)
        grad_w_out = jnp.einsum("td,te->de", attn_low, d_branch, preferred_element_type=jnp.float32)
        d_attended = jnp.einsum(
            "te,de->td", d_branch, full_out, preferred_element_type=jnp.float32
        ).astype(jnp.bfloat16)

        def group_backward(group_items):
            query_group, key_group, value_group, grad_group, log_group = group_items
            scores = scores_of(query_group, key_group, allowed)
            prob_rows = jnp.exp(scores - log_group[..., None])
            grad_prob = jnp.einsum(
                "qhd,khd->hqk", grad_group, value_group, preferred_element_type=jnp.float32
            )
            grad_scores = prob_rows * (
                grad_prob - jnp.sum(prob_rows * grad_prob, -1, keepdims=True)
            )
            grad_raw = (grad_scores * score_scale).astype(jnp.bfloat16)
            grad_query = jnp.einsum(
                "hqk,khd->qhd", grad_raw, key_group, preferred_element_type=jnp.float32
            )
            grad_key = jnp.einsum(
                "hqk,qhd->khd", grad_raw, query_group, preferred_element_type=jnp.float32
            )
            grad_value = jnp.einsum(
                "hqk,qhd->khd",
                prob_rows.astype(jnp.bfloat16),
                grad_group,
                preferred_element_type=jnp.float32,
            )
            return (grad_query, grad_key, grad_value)

        grad_heads = split_heads(d_attended, groups)
        query_part, key_part, value_part = lax.map(
            group_backward, (query_heads, key_heads, value_heads, grad_heads, log_total)
        )
        d_queries = join_heads(query_part).astype(jnp.bfloat16)
        d_key_all = join_heads(key_part)
        d_value_all = join_heads(value_part)
        returned = shifted(
            jnp.stack([d_key_all[:GLOBAL], d_value_all[:GLOBAL]]).astype(jnp.bfloat16), "fsdp", -1
        ).astype(jnp.float32)
        returned = returned * first_block.astype(jnp.float32)
        extra = jnp.pad(returned, ((0, 0), (0, block_rows - GLOBAL), (0, 0)))
        d_keys = (d_key_all[GLOBAL:] + extra[0]).astype(jnp.bfloat16)
        d_values = (d_value_all[GLOBAL:] + extra[1]).astype(jnp.bfloat16)
        grad_b_query = jnp.sum(d_queries, 0, dtype=jnp.float32)
        grad_b_value = jnp.sum(d_values, 0, dtype=jnp.float32)
        grad_w_query = jnp.einsum(
            "td,te->de", normed_low, d_queries, preferred_element_type=jnp.float32
        )
        grad_w_key = jnp.einsum("td,te->de", normed_low, d_keys, preferred_element_type=jnp.float32)
        grad_w_value = jnp.einsum(
            "td,te->de", normed_low, d_values, preferred_element_type=jnp.float32
        )
        d_normed_one = jnp.einsum(
            "te,de->td", d_queries, full_query, preferred_element_type=jnp.float32
        )
        d_normed_one = d_normed_one + jnp.einsum(
            "te,de->td", d_keys, full_key, preferred_element_type=jnp.float32
        )
        d_normed_one = d_normed_one + jnp.einsum(
            "te,de->td", d_values, full_value, preferred_element_type=jnp.float32
        )
        grad_gain_one = jnp.sum(d_normed_one * unit_one, 0)
        grad_shift_one = jnp.sum(d_normed_one, 0)
        grad_inputs = d_middle + normalize_back(d_normed_one, unit_one, inv_one, gain_onef)
        terms = (
            grad_w_query,
            grad_w_key,
            grad_w_value,
            grad_w_out,
            grad_w_up,
            grad_w_down,
            grad_b_query,
            grad_b_value,
            grad_b_out,
            grad_b_up,
            grad_b_down,
            grad_gain_one,
            grad_shift_one,
            grad_gain_two,
            grad_shift_two,
        )
        grad_sum = jax.tree.map(lambda first, second: first + second, grad_sum, terms)
        return (grad_sum, (layer_out, grad_inputs))

    zero_grads = (
        jnp.zeros((D, D), jnp.float32),
        jnp.zeros((D, D), jnp.float32),
        jnp.zeros((D, D), jnp.float32),
        jnp.zeros((D, D), jnp.float32),
        jnp.zeros((D, FF), jnp.float32),
        jnp.zeros((FF, D), jnp.float32),
        jnp.zeros((D,), jnp.float32),
        jnp.zeros((D,), jnp.float32),
        jnp.zeros((D,), jnp.float32),
        jnp.zeros((FF,), jnp.float32),
        jnp.zeros((D,), jnp.float32),
        jnp.zeros((D,), jnp.float32),
        jnp.zeros((D,), jnp.float32),
        jnp.zeros((D,), jnp.float32),
        jnp.zeros((D,), jnp.float32),
    )
    grad_sum, (layer_out, grad_inputs) = lax.scan(
        micro_step, zero_grads, (inputs, cotangent, prefix)
    )
    owned = (
        lax.psum_scatter(grad_sum[0], ("dp", "fsdp"), scatter_dimension=0, tiled=True),
        lax.psum_scatter(grad_sum[1], ("dp", "fsdp"), scatter_dimension=0, tiled=True),
        lax.psum_scatter(grad_sum[2], ("dp", "fsdp"), scatter_dimension=0, tiled=True),
        lax.psum_scatter(grad_sum[3], ("dp", "fsdp"), scatter_dimension=0, tiled=True),
        lax.psum_scatter(grad_sum[4], ("dp", "fsdp"), scatter_dimension=0, tiled=True),
        lax.psum_scatter(grad_sum[5], ("dp", "fsdp"), scatter_dimension=0, tiled=True),
        lax.psum_scatter(grad_sum[6], ("dp", "fsdp"), scatter_dimension=0, tiled=True),
        lax.psum_scatter(grad_sum[7], ("dp", "fsdp"), scatter_dimension=0, tiled=True),
        lax.psum_scatter(grad_sum[8], ("dp", "fsdp"), scatter_dimension=0, tiled=True),
        lax.psum_scatter(grad_sum[9], ("dp", "fsdp"), scatter_dimension=0, tiled=True),
        lax.psum_scatter(grad_sum[10], ("dp", "fsdp"), scatter_dimension=0, tiled=True),
        lax.psum_scatter(grad_sum[11], ("dp", "fsdp"), scatter_dimension=0, tiled=True),
        lax.psum_scatter(grad_sum[12], ("dp", "fsdp"), scatter_dimension=0, tiled=True),
        lax.psum_scatter(grad_sum[13], ("dp", "fsdp"), scatter_dimension=0, tiled=True),
        lax.psum_scatter(grad_sum[14], ("dp", "fsdp"), scatter_dimension=0, tiled=True),
    )
    return (
        layer_out,
        grad_inputs,
        owned[0],
        owned[1],
        owned[2],
        owned[3],
        owned[4],
        owned[5],
        owned[6],
        owned[7],
        owned[8],
        owned[9],
        owned[10],
        owned[11],
        owned[12],
        owned[13],
        owned[14],
    )


def solution(mesh):
    placed = (
        P(None, ("dp", "fsdp"), None),
        P(None, ("dp", "fsdp"), None),
        P(None, "dp"),
        P(("dp", "fsdp"), None),
        P(("dp", "fsdp"), None),
        P(("dp", "fsdp"), None),
        P(("dp", "fsdp"), None),
        P(("dp", "fsdp"), None),
        P(("dp", "fsdp"), None),
        P(("dp", "fsdp")),
        P(("dp", "fsdp")),
        P(("dp", "fsdp")),
        P(("dp", "fsdp")),
        P(("dp", "fsdp")),
        P(("dp", "fsdp")),
        P(("dp", "fsdp")),
        P(("dp", "fsdp")),
        P(("dp", "fsdp")),
    )
    return jax.shard_map(
        body,
        mesh=mesh,
        in_specs=placed,
        out_specs=(
            P(None, ("dp", "fsdp"), None),
            P(None, ("dp", "fsdp"), None),
            P(("dp", "fsdp"), None),
            P(("dp", "fsdp"), None),
            P(("dp", "fsdp"), None),
            P(("dp", "fsdp"), None),
            P(("dp", "fsdp"), None),
            P(("dp", "fsdp"), None),
            P(("dp", "fsdp")),
            P(("dp", "fsdp")),
            P(("dp", "fsdp")),
            P(("dp", "fsdp")),
            P(("dp", "fsdp")),
            P(("dp", "fsdp")),
            P(("dp", "fsdp")),
            P(("dp", "fsdp")),
            P(("dp", "fsdp")),
        ),
        check_vma=False,
    )
```

profile of v0, /device:TPU:0, one launch (start us, length us, event | category | flops | bytes accessed | tf_op | source)
XLA Modules:
  0.0 1766.4 jit_solution(12409645427570794950)
XLA Ops:
  8.2 1048.3 %while.104 = (s32[]{:T(128)}, f32[768,768]{1,0:T(8,128)}, f32[768,768]{1,0:T(8,128)}, f32[768,768]{1,0:T(8,128)}, f32[768,768]{1,0:T(8,128)}, /*index=5*/f32[768...) while((s32[]{:T(128)}, f32[768,768]{1,0:T(8,128)}, ...), condition=%wide.region_26.27_spmd.clone, body=%wide.region_0.26_spmd.clone.sunk | while | flops 22485176320 | bytes 571756288 | solution.py:315
  18.2 42.4 %all-reduce.31 = (bf16[768]{0:T(1024)(128)(2,1)S(1)}, bf16[768]{0:T(1024)(128)(2,1)S(1)}, bf16[768]{0:T(1024)(128)(2,1)S(1)}, bf16[768]{0:T(1024)(128)(2,1)S(1)}...) all-reduce(bf16[768]{0:T(1024)(128)(2,1)S(1)} %dynamic-update-slice, ...), channel_id=1, replica_groups=mesh['dp'=8,'fsdp'=4] {'dp','fsdp'}, use_global_device_ids=true, to_apply=%add.2 | all-reduce | flops 9216 | bytes 36864 | tf_op jit(solution)/shard_map/while
  63.7 5.5 all-gather.9.cloned.1.call-done
  71.5 53.6 %all-gather.7.cloned.1.call-done = bf16[768,768]{1,0:T(8,128)(2,1)} async-done(((bf16[24,768]{1,0:T(8,128)(2,1)}), bf16[768,768]{1,0:T(8,128)(2,1)}) %all-gather.7.cloned.1.call-update) | async-done | bytes 1179664 | tf_op jit(solution)/shard_map/while/body/eval_jaxpr/all_gather | solution.py:90
  128.2 3.2 collective-permute-start
  133.7 47.2 %all-gather.11.cloned.1.call-done = bf16[768,768]{1,0:T(8,128)(2,1)} async-done(((bf16[24,768]{1,0:T(8,128)(2,1)}), bf16[768,768]{1,0:T(8,128)(2,1)}) %all-gather.11.cloned.1.call-update) | async-done | bytes 1179664 | tf_op jit(solution)/shard_map/while/body/eval_jaxpr/all_gather | solution.py:89
  180.9 3.1 add_convert_fusion.16
  190.6 31.3 %while.105 = (s32[]{:T(128)}, bf16[6,512,2,64]{1,3,2,0:T(8,128)(2,1)S(1)}, f32[6,2,512]{2,1,0:T(2,128)}, bf16[6,640,2,64]{1,3,2,0:T(8,128)(2,1)S(1)}, bf16[6,512...) while((s32[]{:T(128)}, ...), condition=%wide.region_7.7_spmd.clone, body=%wide.region_4.6_spmd.clone.sunk | while | flops 176618496 | bytes 9934714 | solution.py:168
  221.9 14.8 all-gather.13.cloned.1.call-done
  239.5 62.6 %all-gather.15.cloned.1.call-done = bf16[768,3072]{1,0:T(8,128)(2,1)} async-done(((bf16[24,3072]{1,0:T(8,128)(2,1)}), bf16[768,3072]{1,0:T(8,128)(2,1)}) %all-gather.15.cloned.1.call-update) | async-done | bytes 4718608 | tf_op jit(solution)/shard_map/while/body/eval_jaxpr/all_gather | solution.py:93
  302.0 7.1 fusion.263
  309.1 58.2 %all-gather.17.cloned.1.call-done = bf16[3072,768]{1,0:T(8,128)(2,1)} async-done(((bf16[96,768]{1,0:T(8,128)(2,1)}), bf16[3072,768]{1,0:T(8,128)(2,1)}) %all-gather.17.cloned.1.call-update) | async-done | bytes 4718608 | tf_op jit(solution)/shard_map/while/body/eval_jaxpr/all_gather | solution.py:94
  367.3 9.7 convert_reduce_fusion.12
  384.1 90.9 %while.106 = (s32[]{:T(128)}, bf16[6,512,2,64]{1,3,2,0:T(8,128)(2,1)S(1)}, f32[6,640,2,64]{1,3,2,0:T(8,128)}, f32[6,640,2,64]{1,3,2,0:T(8,128)}, bf16[6,640,2,64...) while((s32[]{:T(128)}, ...), condition=%wide.region_14.14_spmd.clone, body=%wide.region_12.13_spmd.clone.sunk | while | flops 429591808 | bytes 31445904 | solution.py:244
  391.9 3.3 fusion.288
  395.2 4.0 fusion.289
  407.0 3.3 fusion.288
  410.3 4.0 fusion.289
  422.2 3.3 fusion.288
  425.5 4.0 fusion.289
  437.3 3.3 fusion.288
  440.6 4.0 fusion.289
  452.5 3.3 fusion.288
  455.8 4.0 fusion.289
  467.6 3.3 fusion.288
  470.9 4.0 fusion.289
  478.8 10.4 select_add_fusion.31
  489.3 5.7 select_add_fusion.30
  499.8 8.2 fusion.269
  539.5 42.1 %all-reduce.31 = (bf16[768]{0:T(1024)(128)(2,1)S(1)}, bf16[768]{0:T(1024)(128)(2,1)S(1)}, bf16[768]{0:T(1024)(128)(2,1)S(1)}, bf16[768]{0:T(1024)(128)(2,1)S(1)}...) all-reduce(bf16[768]{0:T(1024)(128)(2,1)S(1)} %dynamic-update-slice, ...), channel_id=1, replica_groups=mesh['dp'=8,'fsdp'=4] {'dp','fsdp'}, use_global_device_ids=true, to_apply=%add.2 | all-reduce | flops 9216 | bytes 36864 | tf_op jit(solution)/shard_map/while
  584.7 3.8 all-gather.9.cloned.1.call-done
  590.7 53.9 %all-gather.7.cloned.1.call-done = bf16[768,768]{1,0:T(8,128)(2,1)} async-done(((bf16[24,768]{1,0:T(8,128)(2,1)}), bf16[768,768]{1,0:T(8,128)(2,1)}) %all-gather.7.cloned.1.call-update) | async-done | bytes 1179664 | tf_op jit(solution)/shard_map/while/body/eval_jaxpr/all_gather | solution.py:90
  647.7 3.4 collective-permute-start
  653.4 47.0 %all-gather.11.cloned.1.call-done = bf16[768,768]{1,0:T(8,128)(2,1)} async-done(((bf16[24,768]{1,0:T(8,128)(2,1)}), bf16[768,768]{1,0:T(8,128)(2,1)}) %all-gather.11.cloned.1.call-update) | async-done | bytes 1179664 | tf_op jit(solution)/shard_map/while/body/eval_jaxpr/all_gather | solution.py:89
  700.5 3.1 add_convert_fusion.16
  710.2 31.3 %while.105 = (s32[]{:T(128)}, bf16[6,512,2,64]{1,3,2,0:T(8,128)(2,1)S(1)}, f32[6,2,512]{2,1,0:T(2,128)}, bf16[6,640,2,64]{1,3,2,0:T(8,128)(2,1)S(1)}, bf16[6,512...) while((s32[]{:T(128)}, ...), condition=%wide.region_7.7_spmd.clone, body=%wide.region_4.6_spmd.clone.sunk | while | flops 176618496 | bytes 9934714 | solution.py:168
  741.5 14.8 all-gather.13.cloned.1.call-done
  759.0 62.7 %all-gather.15.cloned.1.call-done = bf16[768,3072]{1,0:T(8,128)(2,1)} async-done(((bf16[24,3072]{1,0:T(8,128)(2,1)}), bf16[768,3072]{1,0:T(8,128)(2,1)}) %all-gather.15.cloned.1.call-update) | async-done | bytes 4718608 | tf_op jit(solution)/shard_map/while/body/eval_jaxpr/all_gather | solution.py:93
  821.8 7.1 fusion.263
  828.8 58.2 %all-gather.17.cloned.1.call-done = bf16[3072,768]{1,0:T(8,128)(2,1)} async-done(((bf16[96,768]{1,0:T(8,128)(2,1)}), bf16[3072,768]{1,0:T(8,128)(2,1)}) %all-gather.17.cloned.1.call-update) | async-done | bytes 4718608 | tf_op jit(solution)/shard_map/while/body/eval_jaxpr/all_gather | solution.py:94
  887.0 9.3 convert_reduce_fusion.12
  903.4 90.9 %while.106 = (s32[]{:T(128)}, bf16[6,512,2,64]{1,3,2,0:T(8,128)(2,1)S(1)}, f32[6,640,2,64]{1,3,2,0:T(8,128)}, f32[6,640,2,64]{1,3,2,0:T(8,128)}, bf16[6,640,2,64...) while((s32[]{:T(128)}, ...), condition=%wide.region_14.14_spmd.clone, body=%wide.region_12.13_spmd.clone.sunk | while | flops 429591808 | bytes 31445904 | solution.py:244
  911.3 3.3 fusion.288
  914.6 4.0 fusion.289
  926.4 3.3 fusion.288
  929.7 4.0 fusion.289
  941.5 3.3 fusion.288
  944.8 4.0 fusion.289
  956.7 3.3 fusion.288
  960.0 4.0 fusion.289
  971.8 3.3 fusion.288
  975.1 4.0 fusion.289
  987.0 3.3 fusion.288
  990.3 4.0 fusion.289
  998.2 13.1 select_add_fusion.31
  1011.3 8.2 select_add_fusion.30
  1024.3 8.2 fusion.269
  1060.6 42.5 %all-reduce.29 = (f32[768]{0:T(1024)S(1)}, f32[768]{0:T(1024)S(1)}, f32[768]{0:T(1024)S(1)}, f32[3072]{0:T(1024)S(1)}, f32[768]{0:T(1024)S(1)}, /*index=5*/f32[7...) all-reduce(f32[768]{0:T(1024)S(1)} %copy-done.64, ...), channel_id=8, replica_groups=mesh['dp'=8,'fsdp'=4] {'dp','fsdp'}, use_global_device_ids=true, to_apply=%region_33.34.clone | all-reduce | flops 9216 | bytes 73728
  1108.4 54.2 %reduce-scatter.7.cloned.1.call-done = f32[24,768]{1,0:T(8,128)} async-done(((f32[768,768]{1,0:T(8,128)}), f32[24,768]{1,0:T(8,128)}) %reduce-scatter.7.cloned.1.call-update) | async-done | bytes 73744 | tf_op jit(solution)/shard_map/reduce_scatter | solution.py:319
  1162.6 104.5 %reduce-scatter.9.cloned.1.call-done = f32[24,768]{1,0:T(8,128)} async-done(((f32[768,768]{1,0:T(8,128)}), f32[24,768]{1,0:T(8,128)}) %reduce-scatter.9.cloned.1.call-update) | async-done | bytes 73744 | tf_op jit(solution)/shard_map/reduce_scatter | solution.py:320
  1267.1 103.8 %reduce-scatter.11.cloned.1.call-done = f32[24,768]{1,0:T(8,128)} async-done(((f32[768,768]{1,0:T(8,128)}), f32[24,768]{1,0:T(8,128)}) %reduce-scatter.11.cloned.1.call-update) | async-done | bytes 73744 | tf_op jit(solution)/shard_map/reduce_scatter | solution.py:321
  1370.8 104.7 %reduce-scatter.13.cloned.1.call-done = f32[24,768]{1,0:T(8,128)} async-done(((f32[768,768]{1,0:T(8,128)}), f32[24,768]{1,0:T(8,128)}) %reduce-scatter.13.cloned.1.call-update) | async-done | bytes 73744 | tf_op jit(solution)/shard_map/reduce_scatter | solution.py:322
  1475.5 141.2 %reduce-scatter.15.cloned.1.call-done = f32[24,3072]{1,0:T(8,128)} async-done(((f32[768,3072]{1,0:T(8,128)}), f32[24,3072]{1,0:T(8,128)}) %reduce-scatter.15.cloned.1.call-update) | async-done | bytes 294928 | tf_op jit(solution)/shard_map/reduce_scatter | solution.py:323
  1616.7 142.1 %reduce-scatter.17.cloned.1.call-done = f32[96,768]{1,0:T(8,128)} async-done(((f32[3072,768]{1,0:T(8,128)}), f32[96,768]{1,0:T(8,128)}) %reduce-scatter.17.cloned.1.call-update) | async-done | bytes 294928 | tf_op jit(solution)/shard_map/reduce_scatter | solution.py:324
  (686 shorter events, 297.3 us)
Async XLA Ops:
  8.5 8.5 copy-start.77
  8.5 8.7 copy-start.74
  8.6 8.9 copy-start.75
  8.6 9.1 copy-start.82
  8.6 9.4 copy-start.81
  8.6 54.5 %copy-start.67 = (s32[2,2]{1,0:T(2,128)S(1)}, s32[2,2]{1,0:T(2,128)}, u32[]{:S(2)}) copy-start(s32[2,2]{1,0:T(2,128)} %get-tuple-element.1707) | copy-start | bytes 52 | tf_op jit(solution)/shard_map/while
  8.6 60.6 %copy-start = (bf16[2,512,768]{2,1,0:T(8,128)(2,1)S(1)}, bf16[2,512,768]{2,1,0:T(8,128)(2,1)}, u32[]{:S(2)}) copy-start(bf16[2,512,768]{2,1,0:T(8,128)(2,1)} %get-tuple-element.1695) | copy-start | bytes 4718596 | tf_op jit(solution)/shard_map/while
  8.6 60.6 %all-gather.9.cloned.1.call-start = ((), (), s32[]{:S(2)}) async-start(), calls=%async_computation.13 | async-start | bytes 1216512 | tf_op jit(solution)/shard_map/while/body/eval_jaxpr/all_gather | solution.py:91
  9.4 115.7 %all-gather.7.cloned.1.call-start = ((), (), s32[]{:S(2)}) async-start(), calls=%async_computation.12 | async-start | bytes 1216512 | tf_op jit(solution)/shard_map/while/body/eval_jaxpr/all_gather | solution.py:90
  10.1 170.8 %all-gather.11.cloned.1.call-start = ((), (), s32[]{:S(2)}) async-start(), calls=%async_computation.14 | async-start | bytes 1216512 | tf_op jit(solution)/shard_map/while/body/eval_jaxpr/all_gather | solution.py:89
  10.8 225.8 %all-gather.13.cloned.1.call-start = ((), (), s32[]{:S(2)}) async-start(), calls=%async_computation.15 | async-start | bytes 1216512 | tf_op jit(solution)/shard_map/while/body/eval_jaxpr/all_gather | solution.py:92
  11.4 290.6 %all-gather.15.cloned.1.call-start = ((), (), s32[]{:S(2)}) async-start(), calls=%async_computation.16 | async-start | bytes 4866048 | tf_op jit(solution)/shard_map/while/body/eval_jaxpr/all_gather | solution.py:93
  12.0 355.3 %all-gather.17.cloned.1.call-start = ((), (), s32[]{:S(2)}) async-start(), calls=%async_computation.17 | async-start | bytes 4866048 | tf_op jit(solution)/shard_map/while/body/eval_jaxpr/all_gather | solution.py:94
  14.5 166.4 %copy-start.31 = (f32[512]{0:T(512)}, f32[512]{0:T(512)S(1)}, u32[]{:S(2)}) copy-start(f32[512]{0:T(512)S(1)} %broadcast_multiply_fusion.11) | copy-start | bytes 6148 | tf_op jit(solution)/shard_map/while
  16.0 164.9 %copy-start.33 = (f32[512]{0:T(512)}, f32[512]{0:T(512)S(1)}, u32[]{:S(2)}) copy-start(f32[512]{0:T(512)S(1)} %add_rsqrt_fusion.4) | copy-start | bytes 6148 | tf_op jit(solution)/shard_map/while
  60.6 120.3 %copy-start.35 = (f32[768]{0:T(1024)}, f32[768]{0:T(1024)S(1)}, u32[]{:S(2)}) copy-start(f32[768]{0:T(1024)S(1)} %convert_element_type.518) | copy-start | bytes 9220 | tf_op jit(solution)/shard_map/while
  128.2 58.2 %collective-permute-start = (bf16[2,128,768]{2,1,0:T(8,128)(2,1)}, bf16[2,128,768]{2,1,0:T(8,128)(2,1)}, u32[]{:S(2)}, u32[]{:S(2)}) collective-permute-start(bf16[2,128,768]{2,1,0:T(8,128)(2,1)} %pad_maximum_fusion.4), channel_id=1, source_target_pairs={{0,1},{1,2},{2,3},{4,5},{5,6},{6,7},{8,9},{9,10},{10,11},{12,13},{... | collective-permute-start | bytes 1179656 | tf_op jit(solution)/shard_map/while/body/eval_jaxpr/ppermute | solution.py:20
  190.6 46.1 %copy-start.66 = (f32[768]{0:T(1024)S(1)}, f32[768]{0:T(1024)}, u32[]{:S(2)}) copy-start(f32[768]{0:T(1024)} %convert_element_type.522) | copy-start | bytes 9220 | tf_op jit(solution)/shard_map/while
  221.9 14.8 copy-start.15
  221.9 14.8 copy-start.18
  239.1 141.0 %copy-start.2 = (f32[512,768]{1,0:T(8,128)}, f32[512,768]{1,0:T(8,128)S(1)}, u32[]{:S(2)}) copy-start(f32[512,768]{1,0:T(8,128)S(1)} %get-tuple-element.1437) | copy-start | bytes 4718596 | tf_op jit(solution)/shard_map/while
  239.1 62.9 %copy-start.30 = (f32[768]{0:T(1024)S(1)}, f32[768]{0:T(1024)}, u32[]{:S(2)}) copy-start(f32[768]{0:T(1024)} %convert_element_type.524) | copy-start | bytes 9220 | tf_op jit(solution)/shard_map/while
  239.5 127.8 %copy-start.27 = (bf16[2,512,768]{2,1,0:T(8,128)(2,1)S(1)}, bf16[2,512,768]{2,1,0:T(8,128)(2,1)}, u32[]{:S(2)}) copy-start(bf16[2,512,768]{2,1,0:T(8,128)(2,1)} %get-tuple-element.1703) | copy-start | bytes 4718596 | tf_op jit(solution)/shard_map/while
  239.5 127.8 %copy-start.40 = (f32[3072]{0:T(1024)S(1)}, f32[3072]{0:T(1024)}, u32[]{:S(2)}) copy-start(f32[3072]{0:T(1024)} %convert_element_type.525) | copy-start | bytes 36868 | tf_op jit(solution)/shard_map/while
  367.3 9.7 copy-start.68
  477.5 31.9 %collective-permute-start.1 = (bf16[2,128,768]{1,2,0:T(8,128)(2,1)S(1)}, bf16[2,128,768]{1,2,0:T(8,128)(2,1)S(1)}, u32[]{:S(2)}, u32[]{:S(2)}) collective-permute-start(bf16[2,128,768]{1,2,0:T(8,128)(2,1)S(1)} %pad_maximum_fusion.5), channel_id=1, source_target_pairs={{1,0},{2,1},{3,2},{5,4},{6,5},{7,6},{9,8},{10,9},{11,10},{13,12},{... | collective-permute-start | bytes 1179656 | tf_op jit(solution)/shard_map/while/body/eval_jaxpr/ppermute | solution.py:20
  478.8 10.4 copy-start.3
  478.8 10.4 copy-start.17
  529.7 8.4 copy-start.76
  529.7 8.7 copy-start.77
  529.7 8.9 copy-start.74
  529.7 9.1 copy-start.75
  529.7 9.3 copy-start.82
  529.7 9.5 copy-start.81
  529.7 54.4 %copy-start.67 = (s32[2,2]{1,0:T(2,128)S(1)}, s32[2,2]{1,0:T(2,128)}, u32[]{:S(2)}) copy-start(s32[2,2]{1,0:T(2,128)} %get-tuple-element.1707) | copy-start | bytes 52 | tf_op jit(solution)/shard_map/while
  529.7 58.7 %copy-start = (bf16[2,512,768]{2,1,0:T(8,128)(2,1)S(1)}, bf16[2,512,768]{2,1,0:T(8,128)(2,1)}, u32[]{:S(2)}) copy-start(bf16[2,512,768]{2,1,0:T(8,128)(2,1)} %get-tuple-element.1695) | copy-start | bytes 4718596 | tf_op jit(solution)/shard_map/while
  529.8 58.7 %all-gather.9.cloned.1.call-start = ((), (), s32[]{:S(2)}) async-start(), calls=%async_computation.13 | async-start | bytes 1216512 | tf_op jit(solution)/shard_map/while/body/eval_jaxpr/all_gather | solution.py:91
  530.5 114.1 %all-gather.7.cloned.1.call-start = ((), (), s32[]{:S(2)}) async-start(), calls=%async_computation.12 | async-start | bytes 1216512 | tf_op jit(solution)/shard_map/while/body/eval_jaxpr/all_gather | solution.py:90
  531.3 169.2 %all-gather.11.cloned.1.call-start = ((), (), s32[]{:S(2)}) async-start(), calls=%async_computation.14 | async-start | bytes 1216512 | tf_op jit(solution)/shard_map/while/body/eval_jaxpr/all_gather | solution.py:89
  532.0 224.2 %all-gather.13.cloned.1.call-start = ((), (), s32[]{:S(2)}) async-start(), calls=%async_computation.15 | async-start | bytes 1216512 | tf_op jit(solution)/shard_map/while/body/eval_jaxpr/all_gather | solution.py:92
  532.6 289.2 %all-gather.15.cloned.1.call-start = ((), (), s32[]{:S(2)}) async-start(), calls=%async_computation.16 | async-start | bytes 4866048 | tf_op jit(solution)/shard_map/while/body/eval_jaxpr/all_gather | solution.py:93
  533.3 353.7 %all-gather.17.cloned.1.call-start = ((), (), s32[]{:S(2)}) async-start(), calls=%async_computation.17 | async-start | bytes 4866048 | tf_op jit(solution)/shard_map/while/body/eval_jaxpr/all_gather | solution.py:94
  535.8 164.7 %copy-start.31 = (f32[512]{0:T(512)}, f32[512]{0:T(512)S(1)}, u32[]{:S(2)}) copy-start(f32[512]{0:T(512)S(1)} %broadcast_multiply_fusion.11) | copy-start | bytes 6148 | tf_op jit(solution)/shard_map/while
  537.3 163.1 %copy-start.33 = (f32[512]{0:T(512)}, f32[512]{0:T(512)S(1)}, u32[]{:S(2)}) copy-start(f32[512]{0:T(512)S(1)} %add_rsqrt_fusion.4) | copy-start | bytes 6148 | tf_op jit(solution)/shard_map/while
  581.7 118.8 %copy-start.35 = (f32[768]{0:T(1024)}, f32[768]{0:T(1024)S(1)}, u32[]{:S(2)}) copy-start(f32[768]{0:T(1024)S(1)} %convert_element_type.518) | copy-start | bytes 9220 | tf_op jit(solution)/shard_map/while
  647.7 58.2 %collective-permute-start = (bf16[2,128,768]{2,1,0:T(8,128)(2,1)}, bf16[2,128,768]{2,1,0:T(8,128)(2,1)}, u32[]{:S(2)}, u32[]{:S(2)}) collective-permute-start(bf16[2,128,768]{2,1,0:T(8,128)(2,1)} %pad_maximum_fusion.4), channel_id=1, source_target_pairs={{0,1},{1,2},{2,3},{4,5},{5,6},{6,7},{8,9},{9,10},{10,11},{12,13},{... | collective-permute-start | bytes 1179656 | tf_op jit(solution)/shard_map/while/body/eval_jaxpr/ppermute | solution.py:20
  710.2 46.1 %copy-start.66 = (f32[768]{0:T(1024)S(1)}, f32[768]{0:T(1024)}, u32[]{:S(2)}) copy-start(f32[768]{0:T(1024)} %convert_element_type.522) | copy-start | bytes 9220 | tf_op jit(solution)/shard_map/while
  741.5 14.8 copy-start.15
  741.5 14.8 copy-start.18
  758.7 140.8 %copy-start.2 = (f32[512,768]{1,0:T(8,128)}, f32[512,768]{1,0:T(8,128)S(1)}, u32[]{:S(2)}) copy-start(f32[512,768]{1,0:T(8,128)S(1)} %get-tuple-element.1437) | copy-start | bytes 4718596 | tf_op jit(solution)/shard_map/while
  758.7 63.1 %copy-start.30 = (f32[768]{0:T(1024)S(1)}, f32[768]{0:T(1024)}, u32[]{:S(2)}) copy-start(f32[768]{0:T(1024)} %convert_element_type.524) | copy-start | bytes 9220 | tf_op jit(solution)/shard_map/while
  759.0 128.0 %copy-start.27 = (bf16[2,512,768]{2,1,0:T(8,128)(2,1)S(1)}, bf16[2,512,768]{2,1,0:T(8,128)(2,1)}, u32[]{:S(2)}) copy-start(bf16[2,512,768]{2,1,0:T(8,128)(2,1)} %get-tuple-element.1703) | copy-start | bytes 4718596 | tf_op jit(solution)/shard_map/while
  759.0 128.0 %copy-start.40 = (f32[3072]{0:T(1024)S(1)}, f32[3072]{0:T(1024)}, u32[]{:S(2)}) copy-start(f32[3072]{0:T(1024)} %convert_element_type.525) | copy-start | bytes 36868 | tf_op jit(solution)/shard_map/while
  887.0 9.3 copy-start.68
  996.8 37.1 %collective-permute-start.1 = (bf16[2,128,768]{1,2,0:T(8,128)(2,1)S(1)}, bf16[2,128,768]{1,2,0:T(8,128)(2,1)S(1)}, u32[]{:S(2)}, u32[]{:S(2)}) collective-permute-start(bf16[2,128,768]{1,2,0:T(8,128)(2,1)S(1)} %pad_maximum_fusion.5), channel_id=1, source_target_pairs={{1,0},{2,1},{3,2},{5,4},{6,5},{7,6},{9,8},{10,9},{11,10},{13,12},{... | collective-permute-start | bytes 1179656 | tf_op jit(solution)/shard_map/while/body/eval_jaxpr/ppermute | solution.py:20
  998.1 13.1 copy-start.3
  998.2 13.1 copy-start.17
  1011.3 8.3 copy-start.1
  1056.6 106.0 %reduce-scatter.7.cloned.1.call-start = ((), (), s32[]{:S(2)}) async-start(), calls=%async_computation.6 | async-start | bytes 2433024 | tf_op jit(solution)/shard_map/reduce_scatter | solution.py:319
  1057.1 209.9 %reduce-scatter.9.cloned.1.call-start = ((), (), s32[]{:S(2)}) async-start(), calls=%async_computation.7 | async-start | bytes 2433024 | tf_op jit(solution)/shard_map/reduce_scatter | solution.py:320
  1057.7 313.1 %reduce-scatter.11.cloned.1.call-start = ((), (), s32[]{:S(2)}) async-start(), calls=%async_computation.8 | async-start | bytes 2433024 | tf_op jit(solution)/shard_map/reduce_scatter | solution.py:321
  1058.3 417.2 %reduce-scatter.13.cloned.1.call-start = ((), (), s32[]{:S(2)}) async-start(), calls=%async_computation.9 | async-start | bytes 2433024 | tf_op jit(solution)/shard_map/reduce_scatter | solution.py:322
  1059.1 557.7 %reduce-scatter.15.cloned.1.call-start = ((), (), s32[]{:S(2)}) async-start(), calls=%async_computation.10 | async-start | bytes 9732096 | tf_op jit(solution)/shard_map/reduce_scatter | solution.py:323
  1059.8 699.0 %reduce-scatter.17.cloned.1.call-start = ((), (), s32[]{:S(2)}) async-start(), calls=%async_computation.11 | async-start | bytes 9732096 | tf_op jit(solution)/shard_map/reduce_scatter | solution.py:324
  (119 other events, 363.8 us)
Sparse Core Ops, SparseCore 0:
  12.4 56.8 all-gather.8
  72.1 52.8 all-gather.6
  127.9 52.9 all-gather.10
  183.7 52.9 all-gather.12
  239.4 62.5 all-gather.14
  304.8 62.4 all-gather.16
  533.5 54.9 all-gather.8
  591.4 53.1 all-gather.6
  647.5 52.9 all-gather.10
  703.2 52.9 all-gather.12
  759.1 62.5 all-gather.14
  824.5 62.4 all-gather.16
Sparse Core Ops, SparseCore 1:
  1062.9 99.6 reduce-scatter.6
  1169.2 97.9 reduce-scatter.8
  1272.8 98.0 reduce-scatter.10
  1377.6 97.9 reduce-scatter.12
  1482.0 134.6 reduce-scatter.14
  1624.2 134.5 reduce-scatter.16
where the time goes:
time: 1770 us
  waiting for transfers between devices  1140 us (64%)
  matrix products  342 us (19%)
  blocking collectives  127 us (7%)
  other arithmetic  67.1 us (4%)
  local copies, waits for them, and re-layouts  54.7 us (3%)
    reduce_scatter x1, waiting for transfers between devices, body(): lax.psum_scatter(grad_sum[5], ('dp', 'fsdp'), scatter_dimension=0, tiled=...  142 us
    reduce_scatter x1, waiting for transfers between devices, body(): lax.psum_scatter(grad_sum[4], ('dp', 'fsdp'), scatter_dimension=0, tiled=...  141 us
    all_gather x2, waiting for transfers between devices, collect(): lax.all_gather(w_up, ('dp', 'fsdp'), axis=0, tiled=True)  125 us
    all_gather x2, waiting for transfers between devices, collect(): lax.all_gather(w_down, ('dp', 'fsdp'), axis=0, tiled=True)  116 us
    all_gather x2, waiting for transfers between devices, collect(): lax.all_gather(w_key, ('dp', 'fsdp'), axis=0, tiled=True)  107 us
    reduce_scatter x1, waiting for transfers between devices, body(): lax.psum_scatter(grad_sum[3], ('dp', 'fsdp'), scatter_dimension=0, tiled=...  105 us
    reduce_scatter x1, waiting for transfers between devices, body(): lax.psum_scatter(grad_sum[1], ('dp', 'fsdp'), scatter_dimension=0, tiled=...  104 us
    reduce_scatter x1, waiting for transfers between devices, body(): lax.psum_scatter(grad_sum[2], ('dp', 'fsdp'), scatter_dimension=0, tiled=...  104 us
  transfers between devices with their start and end apart: 22, of which 18 were waited for; matrix products, arithmetic and copies ran while one was open for 12% of the time, Pallas kernels for 0%

commit v1 on v0

v1 whole, which is shorter than its diff:
```python
import functools

import jax
import jax.numpy as jnp
from jax import lax
from jax.experimental import pallas as pl
from jax.experimental.pallas import tpu as pltpu
from jax.sharding import PartitionSpec as P

D = 768
FF = 3072
HEADS = 12
GLOBAL = 128
PAIR = 128

norm_epsilon = 1e-05
score_scale = 0.125
log2_e = 1.4426950408889634
masked_fill = -1e30
BOTH = ("dp", "fsdp")
f32 = jnp.float32
bf16 = jnp.bfloat16


def product(left, right):
    return jnp.dot(left, right, preferred_element_type=f32)


def product_t(left, right):
    return lax.dot_general(left, right, (((1,), (1,)), ((), ())), preferred_element_type=f32)


def product_w(left, right):
    return lax.dot_general(left, right, (((0,), (0,)), ((), ())), preferred_element_type=f32)


def normalize(values, gain, shift):
    center = jnp.mean(values, -1, keepdims=True)
    centered = values - center
    spread = jnp.mean(centered * centered, -1, keepdims=True)
    inv_std = lax.rsqrt(spread + norm_epsilon)
    normed = centered * inv_std
    return (normed * gain + shift, normed, inv_std)


def normalize_back(grad_out, normed, inv_std, gain):
    grad_norm = grad_out * gain
    return inv_std * (
        grad_norm
        - jnp.mean(grad_norm, -1, keepdims=True)
        - normed * jnp.mean(grad_norm * normed, -1, keepdims=True)
    )


def lane_half(shape):
    return lax.broadcasted_iota(jnp.int32, shape, 1) < 64


def attend_kernel(info, q_ref, k_ref, v_ref, lk_ref, lv_ref, out_ref, prob_ref, bias_ref):
    micro = pl.program_id(0)
    rows = q_ref.shape[0]

    @pl.when(pl.program_id(1) == 0)
    def _():
        first = info[0] == 1
        prefix_len = jnp.where(first, info[1 + micro], 0)
        query_pos = lax.broadcasted_iota(jnp.int32, (rows, rows), 0)
        key_pos = lax.broadcasted_iota(jnp.int32, (rows, rows), 1)
        allowed = (key_pos <= query_pos) | (key_pos < prefix_len)
        bias_ref[:, GLOBAL:] = jnp.where(allowed, 0.0, masked_fill)
        bias_ref[:, :GLOBAL] = jnp.full((rows, GLOBAL), jnp.where(first, masked_fill, 0.0), f32)

    queries = q_ref[...]
    keys = jnp.concatenate([lk_ref[...], k_ref[...]], 0)
    values = jnp.concatenate([lv_ref[...], v_ref[...]], 0)
    half = lane_half(queries.shape)
    outs = []
    for head in range(2):
        mine = half if head == 0 else jnp.logical_not(half)
        raw = product_t(jnp.where(mine, queries, jnp.zeros_like(queries)), keys)
        scores = raw * (score_scale * log2_e) + bias_ref[...]
        top = jnp.max(scores, -1, keepdims=True)
        expon = jnp.exp2(scores - top)
        total = jnp.sum(expon, -1, keepdims=True)
        prob = (expon * (1.0 / total)).astype(bf16)
        prob_ref[0, head] = prob
        outs.append(product(prob, values))
    out_ref[...] = jnp.where(half, outs[0], outs[1]).astype(bf16)


def attend_back_kernel(
    q_ref, k_ref, v_ref, lk_ref, lv_ref, g_ref, o_ref, prob_ref,
    dq_ref, dk_ref, dv_ref, lead_k_ref, lead_v_ref,
):
    queries = q_ref[...]
    grads = g_ref[...]
    keys = jnp.concatenate([lk_ref[...], k_ref[...]], 0)
    values = jnp.concatenate([lv_ref[...], v_ref[...]], 0)
    half = lane_half(queries.shape)
    half_k = lane_half(keys.shape)
    dot_all = grads.astype(f32) * o_ref[...].astype(f32)
    d_query, d_key, d_value = [], [], []
    for head in range(2):
        mine = half if head == 0 else jnp.logical_not(half)
        grad_head = jnp.where(mine, grads, jnp.zeros_like(grads))
        prob = prob_ref[0, head]
        delta = jnp.sum(jnp.where(mine, dot_all, 0.0), -1, keepdims=True)
        grad_prob = product_t(grad_head, values)
        grad_raw = (prob.astype(f32) * ((grad_prob - delta) * score_scale)).astype(bf16)
        d_query.append(product(grad_raw, keys))
        d_key.append(product_w(grad_raw, queries))
        d_value.append(product_w(prob, grads))
    dq_ref[...] = jnp.where(half, d_query[0], d_query[1]).astype(bf16)
    d_keys = jnp.where(half_k, d_key[0], d_key[1])
    d_values = jnp.where(half_k, d_value[0], d_value[1])
    dk_ref[...] = d_keys[GLOBAL:]
    dv_ref[...] = d_values[GLOBAL:]
    lead_k_ref[...] = d_keys[:GLOBAL].astype(bf16)
    lead_v_ref[...] = d_values[:GLOBAL].astype(bf16)


def attend(info, queries, keys, values, lead, micro, rows):
    pairs = D // PAIR
    tile = lambda m, p, *_: (m, p)
    shifted_tile = lambda m, p, *_: (m, p + pairs)
    row_spec = pl.BlockSpec((rows, PAIR), tile)
    return pl.pallas_call(
        attend_kernel,
        out_shape=(
            jax.ShapeDtypeStruct(queries.shape, bf16),
            jax.ShapeDtypeStruct((micro, HEADS, rows, GLOBAL + rows), bf16),
        ),
        grid_spec=pltpu.PrefetchScalarGridSpec(
            num_scalar_prefetch=1,
            grid=(micro, pairs),
            in_specs=[
                row_spec,
                row_spec,
                row_spec,
                pl.BlockSpec((GLOBAL, PAIR), tile),
                pl.BlockSpec((GLOBAL, PAIR), shifted_tile),
            ],
            out_specs=[
                row_spec,
                pl.BlockSpec((1, 2, rows, GLOBAL + rows), lambda m, p, *_: (m, p, 0, 0)),
            ],
            scratch_shapes=[pltpu.VMEM((rows, GLOBAL + rows), f32)],
        ),
        compiler_params=pltpu.CompilerParams(vmem_limit_bytes=48 << 20),
        name="attend",
    )(info, queries, keys, values, lead, lead)


def attend_back(queries, keys, values, lead, grads, attended, probs, micro, rows):
    pairs = D // PAIR
    tile = lambda m, p: (m, p)
    shifted_tile = lambda m, p: (m, p + pairs)
    row_spec = pl.BlockSpec((rows, PAIR), tile)
    lead_spec = pl.BlockSpec((GLOBAL, PAIR), tile)
    full = queries.shape
    return pl.pallas_call(
        attend_back_kernel,
        out_shape=(
            jax.ShapeDtypeStruct(full, bf16),
            jax.ShapeDtypeStruct(full, f32),
            jax.ShapeDtypeStruct(full, f32),
            jax.ShapeDtypeStruct((micro * GLOBAL, D), bf16),
            jax.ShapeDtypeStruct((micro * GLOBAL, D), bf16),
        ),
        grid=(micro, pairs),
        in_specs=[
            row_spec,
            row_spec,
            row_spec,
            lead_spec,
            pl.BlockSpec((GLOBAL, PAIR), shifted_tile),
            row_spec,
            row_spec,
            pl.BlockSpec((1, 2, rows, GLOBAL + rows), lambda m, p: (m, p, 0, 0)),
        ],
        out_specs=[row_spec, row_spec, row_spec, lead_spec, lead_spec],
        compiler_params=pltpu.CompilerParams(vmem_limit_bytes=48 << 20),
        name="attend_back",
    )(queries, keys, values, lead, lead, grads, attended, probs)


def bits_of(count):
    assert count & (count - 1) == 0
    return count.bit_length() - 1


def swap(value, axis, bit):
    count = lax.axis_size(axis)
    return lax.ppermute(value, axis, [(i, i ^ (1 << bit)) for i in range(count)])


def stage_orders():
    along_f = [("fsdp", b) for b in range(bits_of(lax.axis_size("fsdp")))]
    along_d = [("dp", b) for b in range(bits_of(lax.axis_size("dp")))]
    order_a = along_f + along_d
    order_b = along_f[:1] + along_d[:1] + along_f[1:] + along_d[1:]
    return order_a, order_b


def scatter_sum(terms, order):
    rows, columns = terms.shape[1:]
    bits_f, bits_d = bits_of(lax.axis_size("fsdp")), bits_of(lax.axis_size("dp"))
    names = [("dp", b) for b in reversed(range(bits_d))] + [
        ("fsdp", b) for b in reversed(range(bits_f))
    ]
    held = terms.reshape((2,) * len(names) + (rows, columns))
    for stage in order:
        axis = names.index(stage)
        own = (lax.axis_index(stage[0]) >> stage[1]) & 1
        away = lax.dynamic_index_in_dim(held, 1 - own, axis, keepdims=False).astype(bf16)
        kept = lax.dynamic_index_in_dim(held, own, axis, keepdims=False)
        names = names[:axis] + names[axis + 1 :]
        held = kept + swap(away, *stage).astype(f32)
    return held


def spread_sum(value, order):
    for stage in order:
        value = value + swap(value, *stage)
    return value


def body(
    inputs, cotangent, prefix,
    w_query, w_key, w_value, w_out, w_up, w_down,
    b_query, b_value, b_out, b_up, b_down,
    gain_attn, shift_attn, gain_ffn, shift_ffn,
):
    n_dev = lax.axis_size("dp") * lax.axis_size("fsdp")
    share = w_query.shape[0]
    wide = FF // D
    fsdp_index = lax.axis_index("fsdp")
    own = lax.axis_index("dp") * lax.axis_size("fsdp") + fsdp_index
    first_block = fsdp_index % 2 == 0
    seq_slot = fsdp_index // 2
    micro, rows = inputs.shape[:2]

    vectors = (b_query, b_value, b_out, b_down, gain_attn, shift_attn, gain_ffn, shift_ffn, b_up)
    small = jnp.concatenate(vectors)
    small = jnp.pad(small[None], ((0, 7), (0, D - small.shape[0])))
    pack_one = jnp.concatenate([w_query, w_key, w_value, small], 0)
    pack_two = jnp.concatenate(
        [w_out] + [w_up[:, c * D : (c + 1) * D] for c in range(wide)] + [w_down], 0
    )
    got_one = lax.all_gather(pack_one, BOTH, axis=0)
    got_two = lax.all_gather(pack_two, BOTH, axis=0)

    def unit(got, at):
        return got[:, at * share : (at + 1) * share].reshape(D, D)

    full_query, full_key, full_value = (unit(got_one, i) for i in range(3))
    small_all = got_one[:, 3 * share].astype(f32)
    vector = lambda i: small_all[:, i * share : (i + 1) * share].reshape(D)
    bias_query, bias_value, bias_out, bias_down, gain_one, shift_one, gain_two, shift_two = (
        vector(i) for i in range(8)
    )
    bias_up = small_all[:, 8 * share : (8 + wide) * share].reshape(FF)
    full_out = unit(got_two, 0)
    full_up = jnp.concatenate([unit(got_two, 1 + c) for c in range(wide)], 1)
    full_down = got_two[:, (1 + wide) * share :].reshape(FF, D)

    prefix_len = jnp.sum(jnp.where(jnp.arange(prefix.shape[1]) == seq_slot, prefix, 0), 1)
    info = jnp.concatenate([first_block.astype(jnp.int32)[None], prefix_len.astype(jnp.int32)])

    tokens = inputs.reshape(micro * rows, D)
    grad_out = cotangent.reshape(micro * rows, D)
    values = tokens.astype(f32)
    normed_one, unit_one, inv_one = normalize(values, gain_one, shift_one)
    normed_low = normed_one.astype(bf16)
    queries = (product(normed_low, full_query) + bias_query).astype(bf16)
    key_local = product(normed_low, full_key).astype(bf16)
    value_local = (product(normed_low, full_value) + bias_value).astype(bf16)

    count = lax.axis_size("fsdp")
    pairs_up = [(i, i + 1) for i in range(0, count, 2)]
    pairs_down = [(i + 1, i) for i in range(0, count, 2)]

    def leading(array):
        return array.reshape(micro, rows, D)[:, :GLOBAL].reshape(micro * GLOBAL, D)

    lead = lax.ppermute(
        jnp.concatenate([leading(key_local), leading(value_local)], 1), "fsdp", pairs_up
    )
    attn_low, probs = attend(info, queries, key_local, value_local, lead, micro, rows)

    middle = values + product(attn_low, full_out) + bias_out
    normed_two, unit_two, inv_two = normalize(middle, gain_two, shift_two)
    normed_two_low = normed_two.astype(bf16)
    hidden = product(normed_two_low, full_up) + bias_up
    activated, gelu_back = jax.vjp(jax.nn.gelu, hidden)
    act_low = activated.astype(bf16)
    layer_out = (middle + product(act_low, full_down) + bias_down).astype(bf16)

    grad_outf = grad_out.astype(f32)
    grad_b_down = jnp.sum(grad_outf, 0)
    order_a, order_b = stage_orders()

    def by_owner(array):
        return array.reshape(n_dev, array.shape[0] // n_dev, D)

    grad_w_down = by_owner(product_w(act_low, grad_out))
    half = grad_w_down.shape[1] // 2
    down_a = scatter_sum(grad_w_down[:, :half], order_a)
    down_b = scatter_sum(grad_w_down[:, half:], order_b)
    d_act = product_t(grad_out, full_down)
    d_hidden = gelu_back(d_act)[0].astype(bf16)
    grad_b_up = jnp.sum(d_hidden, 0, dtype=f32)
    up_parts = [
        by_owner(product_w(normed_two_low, d_hidden[:, c * D : (c + 1) * D])) for c in range(wide)
    ]
    up_a = scatter_sum(jnp.concatenate(up_parts[: wide // 2], 1), order_a)
    up_b = scatter_sum(jnp.concatenate(up_parts[wide // 2 :], 1), order_b)
    d_normed_two = product_t(d_hidden, full_up)
    grad_gain_two = jnp.sum(d_normed_two * unit_two, 0)
    grad_shift_two = jnp.sum(d_normed_two, 0)
    d_middle = grad_outf + normalize_back(d_normed_two, unit_two, inv_two, gain_two)
    d_branch = d_middle.astype(bf16)
    grad_b_out = jnp.sum(d_branch, 0, dtype=f32)
    grad_w_out = by_owner(product_w(attn_low, d_branch))
    d_attended = product_t(d_branch, full_out).astype(bf16)

    d_queries, d_key, d_value, lead_k, lead_v = attend_back(
        queries, key_local, value_local, lead, d_attended, attn_low, probs, micro, rows
    )
    returned = lax.ppermute(jnp.concatenate([lead_k, lead_v], 1), "fsdp", pairs_down)
    returned = returned.astype(f32).reshape(micro, GLOBAL, 2 * D)
    extra = jnp.pad(returned, ((0, 0), (0, rows - GLOBAL), (0, 0))).reshape(micro * rows, 2 * D)
    d_keys = (d_key + extra[:, :D]).astype(bf16)
    d_values = (d_value + extra[:, D:]).astype(bf16)
    grad_b_query = jnp.sum(d_queries, 0, dtype=f32)
    grad_b_value = jnp.sum(d_values, 0, dtype=f32)
    out_and_query = jnp.concatenate([grad_w_out, by_owner(product_w(normed_low, d_queries))], 1)
    key_and_value = jnp.concatenate(
        [by_owner(product_w(normed_low, d_keys)), by_owner(product_w(normed_low, d_values))], 1
    )
    attn_a = scatter_sum(out_and_query, order_a)
    attn_b = scatter_sum(key_and_value, order_b)
    d_normed_one = (
        product_t(d_queries, full_query)
        + product_t(d_keys, full_key)
        + product_t(d_values, full_value)
    )
    grad_gain_one = jnp.sum(d_normed_one * unit_one, 0)
    grad_shift_one = jnp.sum(d_normed_one, 0)
    grad_inputs = d_middle + normalize_back(d_normed_one, unit_one, inv_one, gain_one)

    sums = jnp.stack(
        [
            grad_b_query, grad_b_value, grad_b_out, grad_b_down,
            grad_gain_one, grad_shift_one, grad_gain_two, grad_shift_two,
        ]
        + [grad_b_up[c * D : (c + 1) * D] for c in range(wide)]
    )
    sums = spread_sum(sums, order_a)
    owned = lax.dynamic_slice_in_dim(sums[:8], own * share, share, 1)
    owned_up = lax.dynamic_slice_in_dim(sums[8:].reshape(FF), own * share * wide, share * wide, 0)

    up_own = jnp.concatenate(
        [part[c * share : (c + 1) * share] for part in (up_a, up_b) for c in range(wide // 2)], 1
    )
    return (
        layer_out.reshape(micro, rows, D),
        grad_inputs.reshape(micro, rows, D),
        attn_a[share:],
        attn_b[:share],
        attn_b[share:],
        attn_a[:share],
        up_own,
        jnp.concatenate([down_a, down_b], 0),
        owned[0],
        owned[1],
        owned[2],
        owned_up,
        owned[3],
        owned[4],
        owned[5],
        owned[6],
        owned[7],
    )


def solution(mesh):
    tokens = P(None, BOTH, None)
    matrix = P(BOTH, None)
    line = P(BOTH)
    return jax.shard_map(
        body,
        mesh=mesh,
        in_specs=(tokens, tokens, P(None, "dp")) + (matrix,) * 6 + (line,) * 9,
        out_specs=(tokens, tokens) + (matrix,) * 6 + (line,) * 9,
        check_vma=False,
    )
```

time: 1770 us -> 461 us (0.26)
  waiting for transfers between devices: 1140 us -> 145 us
  matrix products: 342 us -> 98 us
  blocking collectives: 127 us -> 0 us
  Pallas kernels: 0 us -> 49.2 us
  other arithmetic: 67.1 us -> 32.1 us
  starting transfers between devices: 9.85 us -> 44.1 us
    reduce_scatter x6 -> x0, waiting for transfers between devices: 650 us -> none  [the longest x1 142 us: body(): lax.psum_scatter(grad_sum[5], ('dp', 'fsdp'), scatter_dimension=0, tiled=...]
    all_gather x12 -> x2, waiting for transfers between devices: 482 us -> 91.6 us  [the longest x1 56.1 us: body(): got_one = lax.all_gather(pack_one, BOTH, axis=0)]
    dot_general x120 -> x21, matrix products: 342 us -> 98 us  [the longest x6 37.9 us: product_t(): lax.dot_general(left, right, (((1,), (1,)), ((), ())), preferred_element_...]
    while x2 -> x0, blocking collectives: 84.6 us -> none
    ppermute x4 -> x37, waiting for transfers between devices: 0.01 us -> 53.6 us  [the longest x35 53.6 us: swap(): return lax.ppermute(value, axis, [(i, i ^ 1 << bit) for i in range(count)])]
    pallas_call x0 -> x2, Pallas kernels: none -> 49.2 us  [the longest x1 25.4 us: attend(): pl.pallas_call(attend_kernel, out_shape=(jax.ShapeDtypeStruct(queries.sha...]
    unnamed x1 -> x0, blocking collectives: 42.5 us -> none
    ppermute x4 -> x37, starting transfers between devices: 9.12 us -> 44 us  [the longest x35 40.3 us: swap(): return lax.ppermute(value, axis, [(i, i ^ 1 << bit) for i in range(count)])]
  transfers between devices with their start and end apart: 22 -> 39, of which waited for: 18 -> 24; matrix products, arithmetic and copies ran while one was open for 12% -> 24% of each run, Pallas kernels for 0% -> 6%
where the time goes in v1:
time: 461 us; the launch traced here: 454 us
  waiting for transfers between devices  145 us (31%)
  matrix products  98 us (21%)
  local copies, waits for them, and re-layouts  69.5 us (15%)
  Pallas kernels  49.2 us (11%)
  starting transfers between devices  44.1 us (10%)
  other arithmetic  32.1 us (7%)
  between operations  15.8 us (3%)
    all_gather x1, waiting for transfers between devices, body(): got_one = lax.all_gather(pack_one, BOTH, axis=0)  56.1 us
    ppermute x35, waiting for transfers between devices, swap(): return lax.ppermute(value, axis, [(i, i ^ 1 << bit) for i in range(count)])  53.6 us
    ppermute x35, starting transfers between devices, swap(): return lax.ppermute(value, axis, [(i, i ^ 1 << bit) for i in range(count)])  40.3 us
    dot_general x6, matrix products, product_t(): lax.dot_general(left, right, (((1,), (1,)), ((), ())), preferred_element_...  37.9 us
    all_gather x1, waiting for transfers between devices, body(): got_two = lax.all_gather(pack_two, BOTH, axis=0)  35.5 us
    dot_general x6, matrix products, product(): return jnp.dot(left, right, preferred_element_type=f32)  31.6 us
    dot_general x9, matrix products, product_w(): lax.dot_general(left, right, (((0,), (0,)), ((), ())), preferred_element_...  28.6 us
    pallas_call x1, Pallas kernels, attend(): pl.pallas_call(attend_kernel, out_shape=(jax.ShapeDtypeStruct(queries.sha...  25.4 us
  transfers between devices with their start and end apart: 39, of which 24 were waited for; matrix products, arithmetic and copies ran while one was open for 24% of the time, Pallas kernels for 6%

profile of v1, /device:TPU:0, one launch (start us, length us, event | category | flops | bytes accessed | tf_op | source)
XLA Modules:
  0.0 453.9 jit_solution(12545999508487874137)
XLA Ops:
  7.2 6.2 %concatenate.53 = bf16[288]{0:T(512)(128)(2,1)S(1)} concatenate(bf16[24]{0:T(256)(128)(2,1)} %param.27, bf16[24]{0:T(256)(128)(2,1)} %param.28, bf16[24]{0:T(256)(128)(2,1)} %param.29, bf16[24]{0:T(256)(128)(2,1)} %param.31, bf16[24]{0:T(256)(128)(2,1)} %param.32, bf16[24]{0:T(256)(128)(2,1)} %param.33, bf16[24]{0:T(256)(128)(2,1)} %param.34, bf16[24]{0:T(256)(128)(2,1)} %param.35, ...), dimensions={0} | concatenate | bytes 1152 | tf_op jit(solution)/shard_map/concatenate | solution.py:244
  20.5 1.7 convert_reduce_fusion.1
  22.9 56.1 %all-gather.5.cloned.1.call-done = bf16[2560,768]{1,0:T(8,128)(2,1)} async-done(((bf16[80,768]{1,0:T(8,128)(2,1)}), bf16[2560,768]{1,0:T(8,128)(2,1)}) %all-gather.5.cloned.1.call-update) | async-done | bytes 3932176 | tf_op jit(solution)/shard_map/all_gather | solution.py:250
  82.3 2.8 fusion.114
  89.1 2.3 collective-permute-start
  101.7 2.8 add_convert_fusion.3.q_ref
  104.6 25.4 %attend.1 = (bf16[1024,768]{1,0:T(8,128)(2,1)S(1)}, bf16[2,12,512,640]{3,2,1,0:T(8,128)(2,1)}) custom-call(s32[3]{0:T(128)S(1)} %pad_add_fusion.info, bf16[1024,768]{1,0:T(8,128)(2,1)S(1)} %add_convert_fusion.3.q_ref, bf16[1024,768]{1,0:T(8,128)(2,1)S(1)} %convolution_convert_fusion.1.k_ref, bf16[1024,768]{1,0:T(8,128)(2,1)} %copy-done.25, ...), custom_call_target="tpu_custom_call" | custom-call | tf_op jit(solution)/shard_map/attend/pallas_call | solution.py:127
  132.2 35.5 %all-gather.7.cloned.1.call-done = bf16[6912,768]{1,0:T(8,128)(2,1)} async-done(((bf16[216,768]{1,0:T(8,128)(2,1)}), bf16[6912,768]{1,0:T(8,128)(2,1)}) %all-gather.7.cloned.1.call-update) | async-done | bytes 10616848 | tf_op jit(solution)/shard_map/all_gather | solution.py:251
  167.7 3.1 fusion.112
  170.8 2.8 slice.239
  174.1 1.6 fusion.121
  176.9 11.9 %fusion.14 = (bf16[3072,1024]{0,1:T(8,128)(2,1)}, f32[1024,3072]{1,0:T(8,128)}) fusion(f32[3072]{0:T(1024)S(1)} %copy-done.57, bf16[1024,768]{1,0:T(8,128)(2,1)S(1)} %add_convert_fusion.1, bf16[768,768]{1,0:T(8,128)(2,1)S(1)} %bitcast.327, bf16[768,768]{1,0:T(8,128)(2,1)S(1)} %bitcast.329, bf16[768,768]{1,0:T(8,128)(2,1)S(1)} %bitcast.331, ...), kind=kOutput, calls=%fused_computation.17 | convolution fusion | flops 4882169856 | bytes 25178112 | tf_op jit(solution)/shard_map/dot_general | solution.py:26
  188.9 17.1 %convert_reduce_fusion = (f32[3072]{0:T(1024)}, bf16[1024,3072]{1,0:T(8,128)(2,1)}) fusion(f32[1024,3072]{1,0:T(8,128)} %get-tuple-element.92, f32[3072]{0:T(1024)S(1)} %copy-done.57, bf16[3072,768]{1,0:T(8,128)(2,1)S(1)} %bitcast.307, bf16[1024,768]{1,0:T(8,128)(2,1)S(1)} %bitcast.306), kind=kOutput, calls=%fused_computation.23 | convolution fusion | flops 4904186880 | bytes 25190400 | tf_op jit(solution)/shard_map/dot_general | solution.py:30
  206.0 9.2 %multiply_reduce_fusion = (f32[768]{0:T(1024)}, f32[1024]{0:T(1024)S(1)}, f32[1024]{0:T(1024)S(1)}, f32[768]{0:T(1024)}, f32[1024,768]{1,0:T(8,128)S(1)}) fusion(f32[1024,768]{1,0:T(8,128)S(1)} %get-tuple-element.89, f32[1024]{0:T(1024)S(1)} %add_rsqrt_fusion, f32[1024]{0:T(1024)S(1)} %broadcast_multiply_fusion.4, f32[768]{0:T(1024)S(1)} %mul.184, ...), kind=kOutput, calls=%fused_computation.68 | convolution fusion | flops 4857786368 | bytes 17327104 | tf_op jit(solution)/shard_map/dot_general | solution.py:30
  215.2 3.0 fusion.53
  218.5 2.9 fusion.51
  221.3 1.5 fusion.57
  222.9 1.5 fusion.55
  224.4 12.5 %add_convert_fusion = bf16[1024,768]{1,0:T(8,128)(2,1)} fusion(f32[1024,768]{1,0:T(8,128)S(1)} %get-tuple-element.89, bf16[3072,768]{1,0:T(8,128)(2,1)S(1)} %bitcast.310, f32[1024,3072]{1,0:T(8,128)} %get-tuple-element.92, f32[3072]{0:T(1024)S(1)} %copy-done.57, f32[768]{0:T(1024)S(1)} %add.375), kind=kOutput, calls=%fused_computation.76 | convolution fusion | flops 4865654784 | bytes 22035456 | tf_op jit(solution)/shard_map/dot_general | solution.py:26
  237.0 1.5 convert_reduce_fusion.3
  238.5 2.6 convolution_convert_fusion.g_ref
  241.1 23.8 %attend_back.1 = (bf16[1024,768]{1,0:T(8,128)(2,1)S(1)}, f32[1024,768]{1,0:T(8,128)}, f32[1024,768]{1,0:T(8,128)}, bf16[256,768]{1,0:T(8,128)(2,1)S(1)}, bf16[256,768]{1,0:T(8,128)(2,1)S(1)}) custom-call(bf16[1024,768]{1,0:T(8,128)(2,1)S(1)} %copy-done.2, bf16[1024,768]{1,0:T(8,128)(2,1)} %copy-done, bf16[1024,768]{1,0:T(8,128)(2,1)} %copy-done.25, ...), custom_call_target="tpu_custom_call" | custom-call | tf_op jit(solution)/shard_map/attend_back/pallas_call | solution.py:161
  267.5 2.0 collective-permute-start.17
  270.6 8.8 %copy.58 = bf16[3072,1024]{1,0:T(8,128)(2,1)} copy(bf16[3072,1024]{0,1:T(8,128)(2,1)} %get-tuple-element.91) | data formatting | bytes 12582912 | tf_op jit(solution)/shard_map/convert_element_type | solution.py:296
  279.4 9.8 %fusion.124 = f32[32,96,768]{2,1,0:T(8,128)} fusion(bf16[32,96,1024]{2,1,0:T(8,128)(2,1)} %bitcast.304, bf16[1024,768,1]{1,0,2:T(8,128)(2,1)} %bitcast.305), kind=kOutput, calls=%fused_computation.265 | convolution fusion | flops 4831838208 | bytes 17301504 | tf_op jit(solution)/shard_map/dot_general | solution.py:34
  289.2 4.6 %fusion.113 = (f32[32,48,768]{2,1,0:T(8,128)S(1)}, f32[32,48,768]{2,1,0:T(8,128)S(1)}) fusion(f32[32,96,768]{2,1,0:T(8,128)} %fusion.124), kind=kLoop, calls=%fused_computation.254 | loop fusion | bytes 18874368 | tf_op jit(solution)/shard_map/slice | solution.py:308
  299.5 3.2 fusion.122
  302.7 2.9 fusion.102
  315.0 4.3 fusion.39
  319.3 2.8 copy.50
  322.1 4.2 fusion.59
  326.9 5.1 %fusion.36 = f32[1024,768]{1,0:T(8,128)} fusion(f32[1024,768]{1,0:T(8,128)} %copy-done.12, bf16[2,512,768]{2,1,0:T(8,128)(2,1)} %param.18, f32[1024,768]{1,0:T(8,128)} %get-tuple-element.43, f32[1024]{0:T(1024)S(1)} %broadcast_multiply_fusion, f32[1024]{0:T(1024)S(1)} %bitcast.340, f32[1024]{0:T(1024)S(1)} %broadcast_multiply_fusion.1, ...), kind=kLoop, calls=%fused_computation.64 | loop fusion | flops 7077888 | bytes 11029504 | tf_op jit(solution)/shard_map/add | solution.py:350
  333.5 1.5 collective-permute-start.33
  337.7 1.5 collective-permute-start.34
  339.9 2.0 collective-permute-done.34
  344.3 1.7 collective-permute-done.35
  346.0 2.1 collective-permute-start.36
  349.3 1.8 collective-permute-done.36
  355.5 2.0 fusion.49
  357.6 1.5 collective-permute-start.18
  359.1 1.7 fusion.50
  362.1 1.5 bitcast_add_fusion.1
  365.0 1.5 bitcast_add_fusion.2
  366.6 7.3 %collective-permute-done.18 = bf16[2,2,2,48,768]{4,3,0,1,2:T(8,128)(2,1)S(1)} collective-permute-done((bf16[2,2,2,48,768]{4,3,0,1,2:T(8,128)(2,1)S(1)}, bf16[2,2,2,48,768]{4,3,0,1,2:T(8,128)(2,1)S(1)}, u32[]{:S(2)}, u32[]{:S(2)}) %collective-permute-start.18) | collective-permute-done | bytes 589856 | tf_op jit(solution)/shard_map/ppermute | solution.py:194
  375.5 1.7 collective-permute-done.13
  378.5 7.1 %collective-permute-done.28 = bf16[2,2,2,48,768]{4,3,0,1,2:T(8,128)(2,1)S(1)} collective-permute-done((bf16[2,2,2,48,768]{4,3,0,1,2:T(8,128)(2,1)S(1)}, bf16[2,2,2,48,768]{4,3,0,1,2:T(8,128)(2,1)S(1)}, u32[]{:S(2)}, u32[]{:S(2)}) %collective-permute-start.28) | collective-permute-done | bytes 589856 | tf_op jit(solution)/shard_map/ppermute | solution.py:194
  385.6 1.5 collective-permute-start.14
  387.3 2.8 collective-permute-done.23
  392.4 2.0 fusion.48
  396.4 1.5 collective-permute-start.8
  398.0 1.5 collective-permute-start.20
  399.6 3.1 collective-permute-done.29
  405.1 1.5 collective-permute-start.25
  406.6 3.7 collective-permute-done.15
  412.7 2.0 collective-permute-start.16
  414.8 2.9 collective-permute-start.31
  422.0 2.5 collective-permute-done.26
  425.9 1.8 collective-permute-start.9
  427.7 4.5 collective-permute-done.4
  432.8 1.8 collective-permute-start.10
  434.5 3.8 collective-permute-done.5
  440.0 1.5 collective-permute-start.11
  441.6 2.3 collective-permute-done.6
  444.6 1.6 collective-permute-done.11
  (335 shorter events, 85.4 us)
Async XLA Ops:
  7.2 15.0 %copy-start.6 = (bf16[2,512,768]{2,1,0:T(8,128)(2,1)S(1)}, bf16[2,512,768]{2,1,0:T(8,128)(2,1)}, u32[]{:S(2)}) copy-start(bf16[2,512,768]{2,1,0:T(8,128)(2,1)} %param.18) | copy-start | bytes 4718596
  7.2 71.8 %all-gather.5.cloned.1.call-start = ((), (), s32[]{:S(2)}) async-start(), calls=%async_computation | async-start | bytes 4055040 | tf_op jit(solution)/shard_map/all_gather | solution.py:250
  15.0 152.8 %all-gather.7.cloned.1.call-start = ((), (), s32[]{:S(2)}) async-start(), calls=%async_computation.1 | async-start | bytes 10948608 | tf_op jit(solution)/shard_map/all_gather | solution.py:251
  82.3 4.3 copy-start.35
  85.2 16.6 %copy-start.41 = (bf16[32,24,768]{2,1,0:T(8,128)(2,1)}, bf16[32,24,768]{2,1,0:T(8,128)(2,1)S(1)}, u32[]{:S(2)}) copy-start(bf16[32,24,768]{2,1,0:T(8,128)(2,1)S(1)} %get-tuple-element.54) | copy-start | bytes 3538948
  88.0 16.5 %copy-start = (bf16[1024,768]{1,0:T(8,128)(2,1)}, bf16[1024,768]{1,0:T(8,128)(2,1)S(1)}, u32[]{:S(2)}) copy-start(bf16[1024,768]{1,0:T(8,128)(2,1)S(1)} %convolution_convert_fusion.1.k_ref) | copy-start | bytes 4718596
  88.1 5.4 %copy-start.61 = (s32[2,2]{1,0:T(2,128)S(1)}, s32[2,2]{1,0:T(2,128)}, u32[]{:S(2)}) copy-start(s32[2,2]{1,0:T(2,128)} %param.20) | copy-start | bytes 52
  89.1 15.5 %collective-permute-start = (bf16[256,1536]{1,0:T(8,128)(2,1)}, bf16[256,1536]{1,0:T(8,128)(2,1)S(1)}, u32[]{:S(2)}, u32[]{:S(2)}) collective-permute-start(bf16[256,1536]{1,0:T(8,128)(2,1)} %pad_maximum_fusion.4), channel_id=1, source_target_pairs={{0,1},{2,3},{4,5},{6,7},{8,9},{10,11},{12,13},{14,15},{16,17},{18,... | collective-permute-start | bytes 2359304 | tf_op jit(solution)/shard_map/ppermute | solution.py:286
  173.6 15.2 %copy-start.28 = (bf16[32,96,768]{2,1,0:T(8,128)(2,1)}, bf16[32,96,768]{2,1,0:T(8,128)(2,1)S(1)}, u32[]{:S(2)}) copy-start(bf16[32,96,768]{2,1,0:T(8,128)(2,1)S(1)} %slice.239) | copy-start | bytes 14155780
  176.9 11.9 %copy-start.27 = (bf16[2,512,768]{2,1,0:T(8,128)(2,1)S(1)}, bf16[2,512,768]{2,1,0:T(8,128)(2,1)}, u32[]{:S(2)}) copy-start(bf16[2,512,768]{2,1,0:T(8,128)(2,1)} %param.19) | copy-start | bytes 4718596
  218.5 47.8 %copy-start.18 = (f32[768,768]{1,0:T(8,128)}, f32[768,768]{1,0:T(8,128)S(1)}, u32[]{:S(2)}) copy-start(f32[768,768]{1,0:T(8,128)S(1)} %fusion.53) | copy-start | bytes 7077892
  222.8 46.6 %copy-start.14 = (f32[768,768]{1,0:T(8,128)}, f32[768,768]{1,0:T(8,128)S(1)}, u32[]{:S(2)}) copy-start(f32[768,768]{1,0:T(8,128)S(1)} %fusion.57) | copy-start | bytes 7077892
  224.4 45.0 %copy-start.16 = (f32[768,768]{1,0:T(8,128)}, f32[768,768]{1,0:T(8,128)S(1)}, u32[]{:S(2)}) copy-start(f32[768,768]{1,0:T(8,128)S(1)} %fusion.55) | copy-start | bytes 7077892
  241.1 25.2 %copy-start.20 = (f32[768,768]{1,0:T(8,128)S(1)}, f32[768,768]{1,0:T(8,128)}, u32[]{:S(2)}) copy-start(f32[768,768]{1,0:T(8,128)} %fusion.51) | copy-start | bytes 7077892
  265.0 40.6 %collective-permute-start.1 = (bf16[256,1536]{1,0:T(8,128)(2,1)S(1)}, bf16[256,1536]{1,0:T(8,128)(2,1)}, u32[]{:S(2)}, u32[]{:S(2)}) collective-permute-start(bf16[256,1536]{1,0:T(8,128)(2,1)S(1)} %pad_maximum_fusion.5), channel_id=1, source_target_pairs={{1,0},{3,2},{5,4},{7,6},{9,8},{11,10},{13,12},{15,14},{17,16},{19,... | collective-permute-start | bytes 2359304 | tf_op jit(solution)/shard_map/ppermute | solution.py:330
  267.5 87.4 %collective-permute-start.17 = (bf16[2,2,2,2,48,768]{5,4,0,1,3,2:T(8,128)(2,1)}, bf16[2,2,2,2,48,768]{5,4,0,1,3,2:T(8,128)(2,1)}, u32[]{:S(2)}, u32[]{:S(2)}) collective-permute-start(bf16[2,2,2,2,48,768]{5,4,0,1,3,2:T(8,128)(2,1)} %fusion.67), channel_id=1, source_target_pairs={{0,1},{1,0},{2,3},{3,2},{4,5},{5,4},{6,7},{7,6},{8,9},{9,8},{10,11... | collective-permute-start | bytes 3538952 | tf_op jit(solution)/shard_map/ppermute | solution.py:194
  270.6 87.0 %collective-permute-start.12 = (bf16[2,2,2,2,48,768]{5,4,0,1,2,3:T(8,128)(2,1)}, bf16[2,2,2,2,48,768]{5,4,0,1,2,3:T(8,128)(2,1)}, u32[]{:S(2)}, u32[]{:S(2)}) collective-permute-start(bf16[2,2,2,2,48,768]{5,4,0,1,2,3:T(8,128)(2,1)} %fusion.66), channel_id=1, source_target_pairs={{0,1},{1,0},{2,3},{3,2},{4,5},{5,4},{6,7},{7,6},{8,9},{9,8},{10,11... | collective-permute-start | bytes 3538952 | tf_op jit(solution)/shard_map/ppermute | solution.py:194
  293.8 9.0 %copy-start.11 = (f32[32,48,768]{2,1,0:T(8,128)}, f32[32,48,768]{2,1,0:T(8,128)S(1)}, u32[]{:S(2)}) copy-start(f32[32,48,768]{2,1,0:T(8,128)S(1)} %get-tuple-element.50) | copy-start | bytes 14155780
  295.1 4.5 copy-start.42
  295.1 65.8 %collective-permute-start.27 = (bf16[2,2,2,2,48,768]{5,4,0,1,3,2:T(8,128)(2,1)}, bf16[2,2,2,2,48,768]{5,4,0,1,3,2:T(8,128)(2,1)}, u32[]{:S(2)}, u32[]{:S(2)}) collective-permute-start(bf16[2,2,2,2,48,768]{5,4,0,1,3,2:T(8,128)(2,1)} %fusion.69), channel_id=1, source_target_pairs={{0,1},{1,0},{2,3},{3,2},{4,5},{5,4},{6,7},{7,6},{8,9},{9,8},{10,11... | collective-permute-start | bytes 3538952 | tf_op jit(solution)/shard_map/ppermute | solution.py:194
  296.4 67.4 %collective-permute-start.22 = (bf16[2,2,2,2,48,768]{5,4,0,1,2,3:T(8,128)(2,1)S(1)}, bf16[2,2,2,2,48,768]{5,4,0,1,2,3:T(8,128)(2,1)}, u32[]{:S(2)}, u32[]{:S(2)}) collective-permute-start(bf16[2,2,2,2,48,768]{5,4,0,1,2,3:T(8,128)(2,1)S(1)} %fusion.68), channel_id=1, source_target_pairs={{0,1},{1,0},{2,3},{3,2},{4,5},{5,4},{6,7},{7,6},{8,9},{9,8},{10,11... | collective-permute-start | bytes 3538952 | tf_op jit(solution)/shard_map/ppermute | solution.py:194
  322.1 4.3 copy-start.52
  326.5 7.0 %collective-permute-start.32 = (f32[12,768]{1,0:T(8,128)S(1)}, f32[12,768]{1,0:T(8,128)S(1)}, u32[]{:S(2)}, u32[]{:S(2)}) collective-permute-start(f32[12,768]{1,0:T(8,128)S(1)} %stack.51), channel_id=1, source_target_pairs={{0,1},{1,0},{2,3},{3,2},{4,5},{5,4},{6,7},{7,6},{8,9},{9,8},{10,11... | collective-permute-start | bytes 110600 | tf_op jit(solution)/shard_map/ppermute | solution.py:194
  326.9 5.2 %copy-start.34 = (bf16[1024,768]{1,0:T(8,128)(2,1)S(1)}, bf16[1024,768]{1,0:T(8,128)(2,1)}, u32[]{:S(2)}) copy-start(bf16[1024,768]{1,0:T(8,128)(2,1)} %copy-done.33) | copy-start | bytes 4718596
  326.9 5.2 %copy-start.36 = (bf16[768,1024]{1,0:T(8,128)(2,1)S(1)}, bf16[768,1024]{1,0:T(8,128)(2,1)}, u32[]{:S(2)}) copy-start(bf16[768,1024]{1,0:T(8,128)(2,1)} %copy.50) | copy-start | bytes 4718596
  333.5 4.2 collective-permute-start.33
  337.7 4.2 collective-permute-start.34
  339.2 8.9 %copy-start.23 = (f32[2,2,2,2,2,24,768]{6,5,4,3,2,1,0:T(8,128)S(1)}, f32[2,2,2,2,2,24,768]{6,5,4,3,2,1,0:T(8,128)}, u32[]{:S(2)}) copy-start(f32[2,2,2,2,2,24,768]{6,5,4,3,2,1,0:T(8,128)} %fusion.59) | copy-start | bytes 7077892
  339.8 9.4 %copy-start.9 = (f32[32,48,768]{2,1,0:T(8,128)}, f32[32,48,768]{2,1,0:T(8,128)S(1)}, u32[]{:S(2)}) copy-start(f32[32,48,768]{2,1,0:T(8,128)S(1)} %pad_maximum_fusion.1) | copy-start | bytes 14155780
  339.8 8.3 %copy-start.21 = (f32[768,768]{1,0:T(8,128)S(1)}, f32[768,768]{1,0:T(8,128)}, u32[]{:S(2)}) copy-start(f32[768,768]{1,0:T(8,128)} %fusion.102) | copy-start | bytes 7077892
  341.8 4.2 collective-permute-start.35
  346.0 5.0 %collective-permute-start.36 = (f32[12,768]{1,0:T(8,128)S(1)}, f32[12,768]{1,0:T(8,128)S(1)}, u32[]{:S(2)}, u32[]{:S(2)}) collective-permute-start(f32[12,768]{1,0:T(8,128)S(1)} %add.432), channel_id=1, source_target_pairs={{0,16},{4,20},{8,24},{12,28},{16,0},{20,4},{24,8},{28,12},{1,17},{... | collective-permute-start | bytes 110600 | tf_op jit(solution)/shard_map/ppermute | solution.py:194
  348.1 7.4 %copy-start.19 = (f32[768,768]{1,0:T(8,128)S(1)}, f32[768,768]{1,0:T(8,128)}, u32[]{:S(2)}) copy-start(f32[768,768]{1,0:T(8,128)} %copy-done.18) | copy-start | bytes 7077892
  351.1 40.7 %collective-permute-start.2 = (bf16[2,2,2,2,48,768]{5,4,3,2,1,0:T(8,128)(2,1)}, bf16[2,2,2,2,48,768]{5,4,3,2,1,0:T(8,128)(2,1)}, u32[]{:S(2)}, u32[]{:S(2)}) collective-permute-start(bf16[2,2,2,2,48,768]{5,4,3,2,1,0:T(8,128)(2,1)} %fusion.70), channel_id=1, source_target_pairs={{0,1},{1,0},{2,3},{3,2},{4,5},{5,4},{6,7},{7,6},{8,9},{9,8},{10,11... | collective-permute-start | bytes 3538952 | tf_op jit(solution)/shard_map/ppermute | solution.py:194
  354.9 39.6 %collective-permute-start.7 = (bf16[2,2,2,2,48,768]{5,4,0,1,3,2:T(8,128)(2,1)}, bf16[2,2,2,2,48,768]{5,4,0,1,3,2:T(8,128)(2,1)S(1)}, u32[]{:S(2)}, u32[]{:S(2)}) collective-permute-start(bf16[2,2,2,2,48,768]{5,4,0,1,3,2:T(8,128)(2,1)} %fusion.65), channel_id=1, source_target_pairs={{0,1},{1,0},{2,3},{3,2},{4,5},{5,4},{6,7},{7,6},{8,9},{9,8},{10,11... | collective-permute-start | bytes 3538952 | tf_op jit(solution)/shard_map/ppermute | solution.py:194
  355.5 6.7 %slice-start.4 = ((s8[4718592]{0:T(1024)(128)(4,1)}), s8[4194304]{0:T(1024)(128)(4,1)S(1)}, s32[]{:S(2)}) async-start(s8[4718592]{0:T(1024)(128)(4,1)} %bitcast.288), calls=%async_computation.6 | async-start | bytes 8388608
  357.6 4.5 slice-start.5
  357.6 16.3 %collective-permute-start.18 = (bf16[2,2,2,48,768]{4,3,0,1,2:T(8,128)(2,1)S(1)}, bf16[2,2,2,48,768]{4,3,0,1,2:T(8,128)(2,1)S(1)}, u32[]{:S(2)}, u32[]{:S(2)}) collective-permute-start(bf16[2,2,2,48,768]{4,3,0,1,2:T(8,128)(2,1)S(1)} %fusion.76), channel_id=1, source_target_pairs={{0,4},{4,0},{8,12},{12,8},{16,20},{20,16},{24,28},{28,24},{1,5},{5... | collective-permute-start | bytes 1769480 | tf_op jit(solution)/shard_map/ppermute | solution.py:194
  359.1 5.8 %slice-start.2 = ((s8[4718592]{0:T(1024)(128)(4,1)}), s8[524288]{0:T(1024)(128)(4,1)S(1)}, s32[]{:S(2)}) async-start(s8[4718592]{0:T(1024)(128)(4,1)} %bitcast.284), calls=%async_computation.4 | async-start | bytes 1048576
  360.9 16.2 %collective-permute-start.13 = (bf16[2,2,2,48,768]{4,3,0,1,2:T(8,128)(2,1)S(1)}, bf16[2,2,2,48,768]{4,3,0,1,2:T(8,128)(2,1)S(1)}, u32[]{:S(2)}, u32[]{:S(2)}) collective-permute-start(bf16[2,2,2,48,768]{4,3,0,1,2:T(8,128)(2,1)S(1)} %fusion.75), channel_id=1, source_target_pairs={{0,2},{1,3},{2,0},{3,1},{4,6},{5,7},{6,4},{7,5},{8,10},{9,11},{10,... | collective-permute-start | bytes 1769480 | tf_op jit(solution)/shard_map/ppermute | solution.py:194
  363.7 21.9 %collective-permute-start.28 = (bf16[2,2,2,48,768]{4,3,0,1,2:T(8,128)(2,1)S(1)}, bf16[2,2,2,48,768]{4,3,0,1,2:T(8,128)(2,1)S(1)}, u32[]{:S(2)}, u32[]{:S(2)}) collective-permute-start(bf16[2,2,2,48,768]{4,3,0,1,2:T(8,128)(2,1)S(1)} %fusion.78), channel_id=1, source_target_pairs={{0,4},{4,0},{8,12},{12,8},{16,20},{20,16},{24,28},{28,24},{1,5},{5... | collective-permute-start | bytes 1769480 | tf_op jit(solution)/shard_map/ppermute | solution.py:194
  373.9 16.3 %collective-permute-start.23 = (bf16[2,2,2,48,768]{4,3,0,1,2:T(8,128)(2,1)S(1)}, bf16[2,2,2,48,768]{4,3,0,1,2:T(8,128)(2,1)S(1)}, u32[]{:S(2)}, u32[]{:S(2)}) collective-permute-start(bf16[2,2,2,48,768]{4,3,0,1,2:T(8,128)(2,1)S(1)} %fusion.77), channel_id=1, source_target_pairs={{0,2},{1,3},{2,0},{3,1},{4,6},{5,7},{6,4},{7,5},{8,10},{9,11},{10,... | collective-permute-start | bytes 1769480 | tf_op jit(solution)/shard_map/ppermute | solution.py:194
  377.1 19.3 %collective-permute-start.19 = (bf16[2,2,48,768]{3,2,0,1:T(8,128)(2,1)S(1)}, bf16[2,2,48,768]{3,2,0,1:T(8,128)(2,1)S(1)}, u32[]{:S(2)}, u32[]{:S(2)}) collective-permute-start(bf16[2,2,48,768]{3,2,0,1:T(8,128)(2,1)S(1)} %fusion.82), channel_id=1, source_target_pairs={{0,2},{1,3},{2,0},{3,1},{4,6},{5,7},{6,4},{7,5},{8,10},{9,11},{10,... | collective-permute-start | bytes 884744 | tf_op jit(solution)/shard_map/ppermute | solution.py:194
  385.6 12.4 %collective-permute-start.14 = (bf16[2,2,48,768]{3,2,0,1:T(8,128)(2,1)S(1)}, bf16[2,2,48,768]{3,2,0,1:T(8,128)(2,1)S(1)}, u32[]{:S(2)}, u32[]{:S(2)}) collective-permute-start(bf16[2,2,48,768]{3,2,0,1:T(8,128)(2,1)S(1)} %fusion.81), channel_id=1, source_target_pairs={{0,4},{4,0},{8,12},{12,8},{16,20},{20,16},{24,28},{28,24},{1,5},{5... | collective-permute-start | bytes 884744 | tf_op jit(solution)/shard_map/ppermute | solution.py:194
  387.1 5.4 %copy-start.24 = (f32[2,2,2,2,2,24,768]{6,5,4,3,2,1,0:T(8,128)S(1)}, f32[2,2,2,2,2,24,768]{6,5,4,3,2,1,0:T(8,128)}, u32[]{:S(2)}) copy-start(f32[2,2,2,2,2,24,768]{6,5,4,3,2,1,0:T(8,128)} %fusion.59) | copy-start | bytes 7077892
  387.2 5.2 %copy-start.22 = (f32[768,768]{1,0:T(8,128)S(1)}, f32[768,768]{1,0:T(8,128)}, u32[]{:S(2)}) copy-start(f32[768,768]{1,0:T(8,128)} %fusion.102) | copy-start | bytes 7077892
  390.1 12.6 %collective-permute-start.29 = (bf16[2,2,48,768]{3,2,0,1:T(8,128)(2,1)S(1)}, bf16[2,2,48,768]{3,2,0,1:T(8,128)(2,1)S(1)}, u32[]{:S(2)}, u32[]{:S(2)}) collective-permute-start(bf16[2,2,48,768]{3,2,0,1:T(8,128)(2,1)S(1)} %fusion.84), channel_id=1, source_target_pairs={{0,2},{1,3},{2,0},{3,1},{4,6},{5,7},{6,4},{7,5},{8,10},{9,11},{10,... | collective-permute-start | bytes 884744 | tf_op jit(solution)/shard_map/ppermute | solution.py:194
  391.8 12.6 %collective-permute-start.24 = (bf16[2,2,48,768]{3,2,0,1:T(8,128)(2,1)S(1)}, bf16[2,2,48,768]{3,2,0,1:T(8,128)(2,1)S(1)}, u32[]{:S(2)}, u32[]{:S(2)}) collective-permute-start(bf16[2,2,48,768]{3,2,0,1:T(8,128)(2,1)S(1)} %fusion.83), channel_id=1, source_target_pairs={{0,4},{4,0},{8,12},{12,8},{16,20},{20,16},{24,28},{28,24},{1,5},{5... | collective-permute-start | bytes 884744 | tf_op jit(solution)/shard_map/ppermute | solution.py:194
  394.5 30.7 %collective-permute-start.3 = (bf16[2,2,2,48,768]{4,3,2,1,0:T(8,128)(2,1)S(1)}, bf16[2,2,2,48,768]{4,3,2,1,0:T(8,128)(2,1)S(1)}, u32[]{:S(2)}, u32[]{:S(2)}) collective-permute-start(bf16[2,2,2,48,768]{4,3,2,1,0:T(8,128)(2,1)S(1)} %fusion.73), channel_id=1, source_target_pairs={{0,2},{1,3},{2,0},{3,1},{4,6},{5,7},{6,4},{7,5},{8,10},{9,11},{10,... | collective-permute-start | bytes 1769480 | tf_op jit(solution)/shard_map/ppermute | solution.py:194
  396.4 29.3 %collective-permute-start.8 = (bf16[2,2,2,48,768]{4,3,0,1,2:T(8,128)(2,1)S(1)}, bf16[2,2,2,48,768]{4,3,0,1,2:T(8,128)(2,1)S(1)}, u32[]{:S(2)}, u32[]{:S(2)}) collective-permute-start(bf16[2,2,2,48,768]{4,3,0,1,2:T(8,128)(2,1)S(1)} %fusion.74), channel_id=1, source_target_pairs={{0,4},{4,0},{8,12},{12,8},{16,20},{20,16},{24,28},{28,24},{1,5},{5... | collective-permute-start | bytes 1769480 | tf_op jit(solution)/shard_map/ppermute | solution.py:194
  398.0 7.0 %collective-permute-start.20 = (bf16[2,48,768]{2,1,0:T(8,128)(2,1)S(1)}, bf16[2,48,768]{2,1,0:T(8,128)(2,1)S(1)}, u32[]{:S(2)}, u32[]{:S(2)}) collective-permute-start(bf16[2,48,768]{2,1,0:T(8,128)(2,1)S(1)} %fusion.89), channel_id=1, source_target_pairs={{0,8},{4,12},{8,0},{12,4},{16,24},{20,28},{24,16},{28,20},{1,9},{5... | collective-permute-start | bytes 442376 | tf_op jit(solution)/shard_map/ppermute | solution.py:194
  402.8 7.6 %collective-permute-start.15 = (bf16[2,48,768]{2,1,0:T(8,128)(2,1)S(1)}, bf16[2,48,768]{2,1,0:T(8,128)(2,1)S(1)}, u32[]{:S(2)}, u32[]{:S(2)}) collective-permute-start(bf16[2,48,768]{2,1,0:T(8,128)(2,1)S(1)} %fusion.88), channel_id=1, source_target_pairs={{0,8},{4,12},{8,0},{12,4},{16,24},{20,28},{24,16},{28,20},{1,9},{5... | collective-permute-start | bytes 442376 | tf_op jit(solution)/shard_map/ppermute | solution.py:194
  404.3 8.4 %collective-permute-start.30 = (bf16[2,48,768]{2,1,0:T(8,128)(2,1)S(1)}, bf16[2,48,768]{2,1,0:T(8,128)(2,1)S(1)}, u32[]{:S(2)}, u32[]{:S(2)}) collective-permute-start(bf16[2,48,768]{2,1,0:T(8,128)(2,1)S(1)} %fusion.91), channel_id=1, source_target_pairs={{0,8},{4,12},{8,0},{12,4},{16,24},{20,28},{24,16},{28,20},{1,9},{5... | collective-permute-start | bytes 442376 | tf_op jit(solution)/shard_map/ppermute | solution.py:194
  405.1 9.7 %collective-permute-start.25 = (bf16[2,48,768]{2,1,0:T(8,128)(2,1)S(1)}, bf16[2,48,768]{2,1,0:T(8,128)(2,1)S(1)}, u32[]{:S(2)}, u32[]{:S(2)}) collective-permute-start(bf16[2,48,768]{2,1,0:T(8,128)(2,1)S(1)} %fusion.90), channel_id=1, source_target_pairs={{0,8},{4,12},{8,0},{12,4},{16,24},{20,28},{24,16},{28,20},{1,9},{5... | collective-permute-start | bytes 442376 | tf_op jit(solution)/shard_map/ppermute | solution.py:194
  410.3 8.9 %collective-permute-start.21 = (bf16[48,768]{1,0:T(8,128)(2,1)S(1)}, bf16[48,768]{1,0:T(8,128)(2,1)S(1)}, u32[]{:S(2)}, u32[]{:S(2)}) collective-permute-start(bf16[48,768]{1,0:T(8,128)(2,1)S(1)} %fusion.96), channel_id=1, source_target_pairs={{0,16},{4,20},{8,24},{12,28},{16,0},{20,4},{24,8},{28,12},{1,17},{... | collective-permute-start | bytes 221192 | tf_op jit(solution)/shard_map/ppermute | solution.py:194
  412.7 7.7 %collective-permute-start.16 = (bf16[48,768]{1,0:T(8,128)(2,1)S(1)}, bf16[48,768]{1,0:T(8,128)(2,1)S(1)}, u32[]{:S(2)}, u32[]{:S(2)}) collective-permute-start(bf16[48,768]{1,0:T(8,128)(2,1)S(1)} %fusion.95), channel_id=1, source_target_pairs={{0,16},{4,20},{8,24},{12,28},{16,0},{20,4},{24,8},{28,12},{1,17},{... | collective-permute-start | bytes 221192 | tf_op jit(solution)/shard_map/ppermute | solution.py:194
  414.8 7.1 %collective-permute-start.31 = (bf16[48,768]{1,0:T(8,128)(2,1)S(1)}, bf16[48,768]{1,0:T(8,128)(2,1)S(1)}, u32[]{:S(2)}, u32[]{:S(2)}) collective-permute-start(bf16[48,768]{1,0:T(8,128)(2,1)S(1)} %fusion.98), channel_id=1, source_target_pairs={{0,16},{4,20},{8,24},{12,28},{16,0},{20,4},{24,8},{28,12},{1,17},{... | collective-permute-start | bytes 221192 | tf_op jit(solution)/shard_map/ppermute | solution.py:194
  419.2 5.3 %collective-permute-start.26 = (bf16[48,768]{1,0:T(8,128)(2,1)S(1)}, bf16[48,768]{1,0:T(8,128)(2,1)S(1)}, u32[]{:S(2)}, u32[]{:S(2)}) collective-permute-start(bf16[48,768]{1,0:T(8,128)(2,1)S(1)} %fusion.97), channel_id=1, source_target_pairs={{0,16},{4,20},{8,24},{12,28},{16,0},{20,4},{24,8},{28,12},{1,17},{... | collective-permute-start | bytes 221192 | tf_op jit(solution)/shard_map/ppermute | solution.py:194
  425.4 6.8 %collective-permute-start.4 = (bf16[2,2,48,768]{3,2,1,0:T(8,128)(2,1)S(1)}, bf16[2,2,48,768]{3,2,1,0:T(8,128)(2,1)S(1)}, u32[]{:S(2)}, u32[]{:S(2)}) collective-permute-start(bf16[2,2,48,768]{3,2,1,0:T(8,128)(2,1)S(1)} %fusion.79), channel_id=1, source_target_pairs={{0,4},{4,0},{8,12},{12,8},{16,20},{20,16},{24,28},{28,24},{1,5},{5... | collective-permute-start | bytes 884744 | tf_op jit(solution)/shard_map/ppermute | solution.py:194
  425.9 6.8 %collective-permute-start.9 = (bf16[2,2,48,768]{3,2,0,1:T(8,128)(2,1)S(1)}, bf16[2,2,48,768]{3,2,0,1:T(8,128)(2,1)S(1)}, u32[]{:S(2)}, u32[]{:S(2)}) collective-permute-start(bf16[2,2,48,768]{3,2,0,1:T(8,128)(2,1)S(1)} %fusion.80), channel_id=1, source_target_pairs={{0,2},{1,3},{2,0},{3,1},{4,6},{5,7},{6,4},{7,5},{8,10},{9,11},{10,... | collective-permute-start | bytes 884744 | tf_op jit(solution)/shard_map/ppermute | solution.py:194
  432.3 6.1 %collective-permute-start.5 = (bf16[2,48,768]{2,1,0:T(8,128)(2,1)S(1)}, bf16[2,48,768]{2,1,0:T(8,128)(2,1)S(1)}, u32[]{:S(2)}, u32[]{:S(2)}) collective-permute-start(bf16[2,48,768]{2,1,0:T(8,128)(2,1)S(1)} %fusion.86), channel_id=1, source_target_pairs={{0,8},{4,12},{8,0},{12,4},{16,24},{20,28},{24,16},{28,20},{1,9},{5... | collective-permute-start | bytes 442376 | tf_op jit(solution)/shard_map/ppermute | solution.py:194
  432.8 7.2 %collective-permute-start.10 = (bf16[2,48,768]{2,1,0:T(8,128)(2,1)S(1)}, bf16[2,48,768]{2,1,0:T(8,128)(2,1)S(1)}, u32[]{:S(2)}, u32[]{:S(2)}) collective-permute-start(bf16[2,48,768]{2,1,0:T(8,128)(2,1)S(1)} %fusion.87), channel_id=1, source_target_pairs={{0,8},{4,12},{8,0},{12,4},{16,24},{20,28},{24,16},{28,20},{1,9},{5... | collective-permute-start | bytes 442376 | tf_op jit(solution)/shard_map/ppermute | solution.py:194
  438.4 5.4 %collective-permute-start.6 = (bf16[48,768]{1,0:T(8,128)(2,1)S(1)}, bf16[48,768]{1,0:T(8,128)(2,1)S(1)}, u32[]{:S(2)}, u32[]{:S(2)}) collective-permute-start(bf16[48,768]{1,0:T(8,128)(2,1)S(1)} %fusion.93), channel_id=1, source_target_pairs={{0,16},{4,20},{8,24},{12,28},{16,0},{20,4},{24,8},{28,12},{1,17},{... | collective-permute-start | bytes 221192 | tf_op jit(solution)/shard_map/ppermute | solution.py:194
  440.0 6.1 %collective-permute-start.11 = (bf16[48,768]{1,0:T(8,128)(2,1)S(1)}, bf16[48,768]{1,0:T(8,128)(2,1)S(1)}, u32[]{:S(2)}, u32[]{:S(2)}) collective-permute-start(bf16[48,768]{1,0:T(8,128)(2,1)S(1)} %fusion.94), channel_id=1, source_target_pairs={{0,16},{4,20},{8,24},{12,28},{16,0},{20,4},{24,8},{28,12},{1,17},{... | collective-permute-start | bytes 221192 | tf_op jit(solution)/shard_map/ppermute | solution.py:194
  (47 other events, 126.5 us)
Sparse Core Ops, SparseCore 0:
  15.1 63.8 all-gather.4
  81.9 85.7 all-gather.6
